TPU v7x, 256 devices: a whole 4x4x8 slice. The times are simulated.
256 devices in a mesh: tm: 64 (over y, z, core), chan: 4 (over x).
Axes of the slice: x: 4, y: 4, z: 8, core: 2. Of those that a mesh axis runs over, the one named last changes fastest.
Arguments:
- signals: bfloat16 [262144, 2048], P('tm', 'chan')
- channel_node: int32 [2048], P('chan'), may hold values from 0 to 127, as said below
- lag_offsets: int32 [8], replicated, may hold values from 0 to 512, as said below
Outputs:
- r_factor: float32 [1024, 1024], replicated
Inputs may be any that keep to these rules, and one draw needn't show every extreme that they name: `channel_node`: every node is named by exactly 16 channels; which channels, and so which channel groups, is drawn. `lag_offsets`: strictly increasing; the first is 0 and the last is 512.
All inputs are finite; a program needn't handle non-finite values.
Results may differ from a plain program's by a relative error of at most 0.0003.
Values sent between devices are 32-bit elements; how exact they have to be, the bound alone decides.
A program may use at most 64 MiB of HBM per device.

v0:
```python
import math

import jax
import jax.numpy as jnp
from jax import lax
from jax.sharding import PartitionSpec as P

NODES = 128
CH = 2048
MAXLAG = 512


def from_behind(value, axis, steps):
    count = lax.axis_size(axis)
    leading, last = (max(0, -steps), min(count, count - steps))
    return lax.ppermute(value, axis, [(source, source + steps) for source in range(leading, last)])


def on_device(signals, channel_node, lag_offsets):
    group_count = lax.axis_size("chan")
    lag_count = lag_offsets.shape[0]
    group_width = NODES // group_count
    onehot = (channel_node[:, None] == jnp.arange(NODES, dtype=jnp.int32)[None, :]).astype(
        jnp.bfloat16
    )
    partial_value = jnp.dot(signals, onehot, preferred_element_type=jnp.float32)
    node_scale = 1.0 / math.sqrt(CH // NODES)
    node_share = (
        lax.psum_scatter(partial_value, "chan", scatter_dimension=1, tiled=True) * node_scale
    )
    rim_rows = from_behind(node_share[:MAXLAG], "tm", -1)
    extended = jnp.concatenate([node_share, rim_rows], axis=0)
    time_rows = node_share.shape[0]
    columns = []
    for lag_index in range(lag_count):
        columns.append(
            lax.dynamic_slice(
                extended, (lag_offsets[lag_index], jnp.int32(0)), (time_rows, group_width)
            )
        )
    panel = jnp.concatenate(columns, axis=1)
    hankel = lax.all_to_all(panel, "chan", split_axis=0, concat_axis=1, tiled=True)
    row_total = hankel.shape[0] * lax.axis_size("tm") * group_count
    local_gram = lax.dot_general(
        hankel,
        hankel,
        (((0,), (0,)), ((), ())),
        precision=lax.Precision.HIGHEST,
        preferred_element_type=jnp.float32,
    )
    gram_matrix = lax.psum(local_gram, ("tm", "chan"))
    return jnp.linalg.cholesky(gram_matrix / row_total).T


def solution(mesh):
    in_specs = (P("tm", "chan"), P("chan"), P())
    out_specs = P()
    return jax.shard_map(
        on_device, mesh=mesh, in_specs=in_specs, out_specs=out_specs, check_vma=False
    )
```

profile of v0, /device:TPU:1, one launch (start us, length us, event | category | flops | bytes accessed | tf_op | source)
XLA Modules:
  0.0 641.3 jit_solution(7835683541833374549)
XLA Ops:
  6.5 5.2 convolution_bitcast_fusion
  11.8 36.2 %reduce-scatter.2.cloned.1.call-done = f32[4096,32]{0,1:T(8,128)} async-done(((f32[4096,128]{0,1:T(8,128)}), f32[4096,32]{0,1:T(8,128)}) %reduce-scatter.2.cloned.1.call-update) | async-done | bytes 524304 | tf_op jit(solution)/shard_map/reduce_scatter | solution.py:29
  49.0 2.5 collective-permute-start
  70.5 51.9 %all_to_all.19 = f32[4,1024,256]{1,2,0:T(8,128)S(1)} all-to-all(f32[4,1024,256]{1,2,0:T(8,128)S(1)} %bitcast.64), channel_id=1, replica_groups=mesh['tm'=64,'chan'=4] {'chan'}, dimensions={0} | all-to-all | bytes 8388608 | tf_op jit(solution)/shard_map/all_to_all | solution.py:42
  122.4 14.9 %fusion.48 = f32[1024,1024]{0,1:T(8,128)} fusion(f32[1024,1024]{0,1:T(8,128)S(1)} %bitcast.66), kind=kOutput, calls=%fused_computation.117 | convolution fusion | flops 12884901888 | bytes 8388608 | tf_op jit(solution)/shard_map/dot_general | solution.py:44
  137.3 266.6 %all-reduce.3.cloned.1.call-done = f32[1024,1024]{0,1:T(8,128)} async-done(((f32[1024,1024]{0,1:T(8,128)}), f32[1024,1024]{0,1:T(8,128)}) %all-reduce.3.cloned.1.call-update) | async-done | bytes 4194320 | tf_op jit(solution)/shard_map/psum | solution.py:51
  403.9 5.0 broadcast_multiply_fusion
  408.9 5.8 copy.9
  414.8 4.4 fusion
  421.2 11.7 %cholesky.223 = f32[128,128]{1,0:T(8,128)S(1)} custom-call(f32[128,128]{1,0:T(8,128)S(1)} %cholesky.580), custom_call_target="Cholesky" | custom-call | tf_op jit(solution)/shard_map/jit(cholesky)/cholesky | solution.py:52
  432.9 9.8 %custom-call.59 = f32[1,128,128]{1,2,0:T(8,128)S(1)} custom-call(f32[1,128,128]{2,1,0:T(8,128)S(1)} %get-tuple-element.26), custom_call_target="InvertDiagBlocksLowerTriangular" | custom-call | tf_op jit(solution)/shard_map/jit(cholesky)/cholesky | solution.py:52
  442.8 2.5 cholesky.255
  445.3 2.3 constant_dynamic-update-slice_fusion
  449.2 11.9 %cholesky.244 = f32[128,128]{1,0:T(8,128)S(1)} custom-call(f32[128,128]{1,0:T(8,128)S(1)} %cholesky.584), custom_call_target="Cholesky" | custom-call | tf_op jit(solution)/shard_map/jit(cholesky)/cholesky | solution.py:52
  461.7 9.8 %custom-call.60 = f32[1,128,128]{1,2,0:T(8,128)S(1)} custom-call(f32[1,128,128]{2,1,0:T(8,128)S(1)} %get-tuple-element.23), custom_call_target="InvertDiagBlocksLowerTriangular" | custom-call | tf_op jit(solution)/shard_map/jit(cholesky)/cholesky | solution.py:52
  472.7 2.1 convolution_subtract_fusion.1
  474.8 11.7 %cholesky.468 = f32[128,128]{1,0:T(8,128)S(1)} custom-call(f32[128,128]{1,0:T(8,128)S(1)} %cholesky.589), custom_call_target="Cholesky" | custom-call | tf_op jit(solution)/shard_map/jit(cholesky)/cholesky | solution.py:52
  487.8 9.8 %custom-call.61 = f32[1,128,128]{1,2,0:T(8,128)S(1)} custom-call(f32[1,128,128]{2,1,0:T(8,128)S(1)} %get-tuple-element.20), custom_call_target="InvertDiagBlocksLowerTriangular" | custom-call | tf_op jit(solution)/shard_map/jit(cholesky)/cholesky | solution.py:52
  498.8 2.3 convolution_subtract_fusion.2
  501.1 11.9 %cholesky.487 = f32[128,128]{1,0:T(8,128)S(1)} custom-call(f32[128,128]{1,0:T(8,128)S(1)} %cholesky.594), custom_call_target="Cholesky" | custom-call | tf_op jit(solution)/shard_map/jit(cholesky)/cholesky | solution.py:52
  514.3 9.8 %custom-call.62 = f32[1,128,128]{1,2,0:T(8,128)S(1)} custom-call(f32[1,128,128]{2,1,0:T(8,128)S(1)} %get-tuple-element.17), custom_call_target="InvertDiagBlocksLowerTriangular" | custom-call | tf_op jit(solution)/shard_map/jit(cholesky)/cholesky | solution.py:52
  525.2 2.4 convolution_subtract_fusion.3
  527.6 11.7 %cholesky.506 = f32[128,128]{1,0:T(8,128)S(1)} custom-call(f32[128,128]{1,0:T(8,128)S(1)} %cholesky.599), custom_call_target="Cholesky" | custom-call | tf_op jit(solution)/shard_map/jit(cholesky)/cholesky | solution.py:52
  540.7 10.2 %custom-call.63 = f32[1,128,128]{1,2,0:T(8,128)S(1)} custom-call(f32[1,128,128]{2,1,0:T(8,128)S(1)} %get-tuple-element.14), custom_call_target="InvertDiagBlocksLowerTriangular" | custom-call | tf_op jit(solution)/shard_map/jit(cholesky)/cholesky | solution.py:52
  551.9 2.3 convolution_subtract_fusion.4
  554.2 11.7 %cholesky.526 = f32[128,128]{1,0:T(8,128)S(1)} custom-call(f32[128,128]{1,0:T(8,128)S(1)} %cholesky.604), custom_call_target="Cholesky" | custom-call | tf_op jit(solution)/shard_map/jit(cholesky)/cholesky | solution.py:52
  567.2 9.8 %custom-call.64 = f32[1,128,128]{1,2,0:T(8,128)S(1)} custom-call(f32[1,128,128]{2,1,0:T(8,128)S(1)} %get-tuple-element.11), custom_call_target="InvertDiagBlocksLowerTriangular" | custom-call | tf_op jit(solution)/shard_map/jit(cholesky)/cholesky | solution.py:52
  579.9 11.9 %cholesky.546 = f32[128,128]{1,0:T(8,128)S(1)} custom-call(f32[128,128]{1,0:T(8,128)S(1)} %cholesky.609), custom_call_target="Cholesky" | custom-call | tf_op jit(solution)/shard_map/jit(cholesky)/cholesky | solution.py:52
  593.1 9.8 %custom-call.65 = f32[1,128,128]{1,2,0:T(8,128)S(1)} custom-call(f32[1,128,128]{2,1,0:T(8,128)S(1)} %get-tuple-element.8), custom_call_target="InvertDiagBlocksLowerTriangular" | custom-call | tf_op jit(solution)/shard_map/jit(cholesky)/cholesky | solution.py:52
  605.5 11.7 %cholesky.564 = f32[128,128]{1,0:T(8,128)S(1)} custom-call(f32[128,128]{1,0:T(8,128)S(1)} %convolution_subtract_fusion.6), custom_call_target="Cholesky" | custom-call | tf_op jit(solution)/shard_map/jit(cholesky)/cholesky | solution.py:52
  624.2 4.8 select_bitcast_fusion
  628.9 5.3 copy.10
  (52 shorter events, 27.9 us)
Async XLA Ops:
  6.5 45.0 %copy-start.1 = (s32[8]{0:T(128)S(1)}, s32[8]{0:T(128)}, u32[]{:S(2)}) copy-start(s32[8]{0:T(128)} %param.5) | copy-start | bytes 100
  6.5 41.4 %reduce-scatter.2.cloned.1.call-start = ((), (), s32[]{:S(2)}) async-start(), calls=%async_computation.2 | async-start | bytes 2621440 | tf_op jit(solution)/shard_map/reduce_scatter | solution.py:29
  11.7 392.2 %all-reduce.3.cloned.1.call-start = ((), (), s32[]{:S(2)}) async-start(), calls=%async_computation.3 | async-start | bytes 8388608 | tf_op jit(solution)/shard_map/psum | solution.py:51
  49.0 18.1 %collective-permute-start = (f32[512,32]{0,1:T(8,128)S(1)}, f32[512,32]{0,1:T(8,128)S(1)}, u32[]{:S(2)}, u32[]{:S(2)}) collective-permute-start(f32[512,32]{0,1:T(8,128)S(1)} %slice.213), channel_id=1, source_target_pairs={{4,0},{8,4},{12,8},{16,12},{20,16},{24,20},{28,24},{32,28},{36,32}... | collective-permute-start | bytes 196616 | tf_op jit(solution)/shard_map/ppermute | solution.py:16
  419.3 1.9 copy-start
Sparse Core Ops, SparseCore 0:
  11.8 36.0 reduce-scatter.1
  137.4 266.4 all-reduce.2
where the time goes:
time: 647 us; the launch traced here: 641 us
  waiting for transfers between devices  303 us (47%)
  other arithmetic  190 us (29%)
  blocking collectives  51.9 us (8%)
  matrix products  43 us (7%)
  between operations  33.6 us (5%)
  local copies, waits for them, and re-layouts  16.9 us (3%)
    psum x1, waiting for transfers between devices, on_device(): gram_matrix = lax.psum(local_gram, ('tm', 'chan'))  267 us
    another operation x30, other arithmetic, on_device(): return jnp.linalg.cholesky(gram_matrix / row_total).T  172 us
    all_to_all x1, blocking collectives, on_device(): lax.all_to_all(panel, 'chan', split_axis=0, concat_axis=1, tiled=True)  51.9 us
    reduce_scatter x1, waiting for transfers between devices, on_device(): lax.psum_scatter(partial_value, 'chan', scatter_dimension=1, tiled=True)  36.2 us
    another operation x14, matrix products, on_device(): return jnp.linalg.cholesky(gram_matrix / row_total).T  22.9 us
    dot_general x1, matrix products, on_device(): lax.dot_general(hankel, hankel, (((0,), (0,)), ((), ())), precision=lax.P...  14.9 us
  transfers between devices with their start and end apart: 3, of which 2 were waited for; matrix products, arithmetic and copies ran while one was open for 0% of the time, Pallas kernels for 0%

commit v1 on v0

v1 whole, which is shorter than its diff:
```python
import functools
import math

import jax
import jax.numpy as jnp
from jax import lax
from jax.experimental import pallas as pl
from jax.experimental.pallas import tpu as pltpu
from jax.sharding import PartitionSpec as P

NODES = 128
CH = 2048
MAXLAG = 512

def lanes(x, c):
    return jnp.broadcast_to(x[:, c:c+1], x.shape)

def subs(x, r):
    return jnp.broadcast_to(x[r:r+1, :], x.shape)

def factor_block(rows, nb):
    count = nb // 8
    lane = lax.broadcasted_iota(jnp.int32, (8, nb), 1)
    sub = lax.broadcasted_iota(jnp.int32, (8, nb), 0)
    rows = list(rows)
    inv = [jnp.where(lane == sub + 8 * i, 1.0, 0.0).astype(jnp.float32) for i in range(count)]
    for p in range(count):
        r0 = 8 * p
        col = [[None] * count for _ in range(8)]
        for j in range(8):
            for b in range(p, count):
                col[j][b] = lanes(rows[b], r0 + j)
        e = [[None] * 8 for _ in range(8)]
        for i in range(8):
            for j in range(i, 8):
                e[i][j] = subs(col[i][p], j)
        rinv = [None] * 8
        for j in range(8):
            rinv[j] = 1.0 / e[j][j]
            for i in range(j + 1, 8):
                for k in range(i, 8):
                    e[i][k] = e[i][k] - (e[j][i] * e[j][k]) * rinv[j]
        diag = e[7][7]
        for j in range(7):
            diag = jnp.where(sub == j, e[j][j], diag)
        rs = lax.rsqrt(diag)
        for b in range(p, count):
            for j in range(8):
                v = col[j][b]
                for i in range(j):
                    v = v - col[i][b] * e[i][j]
                v = v * rinv[j]
                if b == p:
                    v = jnp.where(sub > j, v, 0.0)
                col[j][b] = v
        for j in range(8):
            ra, rw = subs(rows[p], j), subs(inv[p], j)
            for b in range(p, count):
                rows[b] = rows[b] - col[j][b] * ra
                inv[b] = inv[b] - col[j][b] * rw
        rows[p] = jnp.where(lane >= sub + r0, rows[p] * rs, 0.0)
        inv[p] = inv[p] * rs
    return rows, inv

DOT = dict(precision=lax.Precision.HIGHEST, preferred_element_type=jnp.float32)

def chol_body(n, nb, scale, g_ref, r_ref, w_ref, d_ref):
    nblk = n // nb
    r_ref[...] = jnp.zeros_like(r_ref)

    def update(k):
        r0 = k * nb
        if k == 0:
            v = g_ref[0:nb, :] * scale
        else:
            v = g_ref[r0:r0+nb, r0:] * scale - lax.dot_general(
                r_ref[0:r0, r0:r0+nb], r_ref[0:r0, r0:], (((0,), (0,)), ((), ())), **DOT)
        r_ref[r0:r0+nb, r0:] = v
        d_ref[...] = v[:, :nb]

    def panel(k):
        r0 = k * nb
        r_ref[r0:r0+nb, r0:r0+nb] = d_ref[...]
        if k + 1 < nblk:
            r_ref[r0:r0+nb, r0+nb:] = lax.dot_general(
                w_ref[...], r_ref[r0:r0+nb, r0+nb:], (((1,), (0,)), ((), ())), **DOT)

    def step(k, _):
        lax.switch(k, [functools.partial(update, i) for i in range(nblk)])
        rows, inv = factor_block([d_ref[8*i:8*i+8, :] for i in range(nb // 8)], nb)
        for i in range(nb // 8):
            d_ref[8*i:8*i+8, :] = rows[i]
            w_ref[8*i:8*i+8, :] = inv[i]
        lax.switch(k, [functools.partial(panel, i) for i in range(nblk)])
        return 0
    lax.fori_loop(0, nblk, step, 0)

def cholesky_r(g, scale):
    n = g.shape[0]
    nb = 128
    return pl.pallas_call(
        functools.partial(chol_body, n, nb, scale),
        out_shape=jax.ShapeDtypeStruct((n, n), jnp.float32),
        in_specs=[pl.BlockSpec(memory_space=pltpu.VMEM)],
        out_specs=pl.BlockSpec(memory_space=pltpu.VMEM),
        scratch_shapes=[pltpu.VMEM((nb, nb), jnp.float32)] * 2,
        compiler_params=pltpu.CompilerParams(vmem_limit_bytes=48 << 20),
    )(g)


def on_device(signals, channel_node, lag_offsets):
    axes = ("tm", "chan")
    parts = lax.axis_size("tm") * lax.axis_size("chan")
    groups = lax.axis_size("chan")
    lag_count = lag_offsets.shape[0]
    width = NODES // groups
    node_scale = 1.0 / math.sqrt(CH // NODES)
    onehot = (channel_node[:, None] == jnp.arange(NODES, dtype=jnp.int32)[None, :]).astype(
        jnp.bfloat16
    )
    partial_sum = jnp.dot(signals, onehot, preferred_element_type=jnp.float32)
    node_rows = lax.psum_scatter(partial_sum, "chan", scatter_dimension=0, tiled=True) * node_scale
    halo = lax.ppermute(node_rows[:MAXLAG], axes, [(i, i - 1) for i in range(1, parts)])
    extended = jnp.concatenate([node_rows, halo], axis=0)
    rows = node_rows.shape[0]
    columns = []
    for group in range(groups):
        for lag_index in range(lag_count):
            columns.append(
                lax.dynamic_slice(
                    extended, (lag_offsets[lag_index], jnp.int32(group * width)), (rows, width)
                )
            )
    hankel = jnp.concatenate(columns, axis=1)
    local_gram = lax.dot_general(
        hankel,
        hankel,
        (((0,), (0,)), ((), ())),
        precision=lax.Precision.HIGHEST,
        preferred_element_type=jnp.float32,
    )
    gram = lax.psum(local_gram, axes)
    return cholesky_r(gram, 1.0 / (rows * parts))


def solution(mesh):
    in_specs = (P("tm", "chan"), P("chan"), P())
    out_specs = P()
    return jax.shard_map(
        on_device, mesh=mesh, in_specs=in_specs, out_specs=out_specs, check_vma=False
    )
```

time: 647 us -> 414 us (0.64)
  other arithmetic: 190 us -> 5.69 us
  blocking collectives: 51.9 us -> 0 us
  Pallas kernels: 0 us -> 49.8 us
  matrix products: 43 us -> 19.9 us
  local copies, waits for them, and re-layouts: 16.9 us -> 2.89 us
    another operation x30 -> x0, other arithmetic: 172 us -> none  [on_device(): return jnp.linalg.cholesky(gram_matrix / row_total).T]
    all_to_all x1 -> x0, blocking collectives: 51.9 us -> none  [on_device(): lax.all_to_all(panel, 'chan', split_axis=0, concat_axis=1, tiled=True)]
    pallas_call x0 -> x1, Pallas kernels: none -> 49.8 us  [cholesky_r(): pl.pallas_call(functools.partial(chol_body, n, nb, scale), out_shape=jax....]
    another operation x14 -> x0, matrix products: 22.9 us -> none  [on_device(): return jnp.linalg.cholesky(gram_matrix / row_total).T]
    div x2 -> x0, other arithmetic: 9.49 us -> none  [on_device(): return jnp.linalg.cholesky(gram_matrix / row_total).T]
where the time goes in v1:
time: 414 us; the launch traced here: 413 us
  waiting for transfers between devices  303 us (73%)
  Pallas kernels  49.8 us (12%)
  between operations  28.7 us (7%)
  matrix products  19.9 us (5%)
  other arithmetic  5.69 us (1%)
    psum x1, waiting for transfers between devices, on_device(): gram = lax.psum(local_gram, axes)  267 us
    pallas_call x1, Pallas kernels, cholesky_r(): pl.pallas_call(functools.partial(chol_body, n, nb, scale), out_shape=jax....  49.8 us
    reduce_scatter x1, waiting for transfers between devices, on_device(): lax.psum_scatter(partial_sum, 'chan', scatter_dimension=0, tiled=True)  36.2 us
    dot_general x1, matrix products, on_device(): lax.dot_general(hankel, hankel, (((0,), (0,)), ((), ())), precision=lax.P...  14.7 us
  transfers between devices with their start and end apart: 3, of which 2 were waited for; matrix products, arithmetic and copies ran while one was open for 0% of the time, Pallas kernels for 0%

profile of v1, /device:TPU:1, one launch (start us, length us, event | category | flops | bytes accessed | tf_op | source)
XLA Modules:
  0.0 412.9 jit_solution(9046236808396886715)
XLA Ops:
  6.5 5.2 %convolution_bitcast_fusion = f32[4096,128]{0,1:T(8,128)} fusion(bf16[4096,512]{1,0:T(8,128)(2,1)} %param.3, s32[512]{0:T(512)} %param.4), kind=kOutput, calls=%fused_computation.32 | convolution fusion | flops 537001984 | bytes 6293504 | tf_op jit(solution)/shard_map/dot_general | solution.py:121
  11.8 36.2 %reduce-scatter.2.cloned.1.call-done = f32[1024,128]{0,1:T(8,128)} async-done(((f32[4096,128]{0,1:T(8,128)}), f32[1024,128]{0,1:T(8,128)}) %reduce-scatter.2.cloned.1.call-update) | async-done | bytes 524304 | tf_op jit(solution)/shard_map/reduce_scatter | solution.py:122
  48.0 1.1 broadcast_multiply_fusion
  49.1 3.0 collective-permute-start
  52.1 0.7 fusion.67
  68.0 0.1 fusion.7
  68.1 0.1 fusion.9
  68.3 0.1 fusion.11
  68.4 0.1 fusion.13
  68.6 0.1 fusion.15
  68.7 0.1 fusion.17
  68.9 0.1 fusion.19
  69.0 0.1 fusion.21
  69.2 0.1 fusion.23
  69.3 0.1 fusion.25
  69.5 0.1 fusion.27
  69.6 0.1 fusion.29
  69.8 0.1 fusion.31
  70.2 0.1 fusion.37
  70.4 0.1 fusion.39
  70.5 0.1 fusion.41
  70.7 0.1 fusion.43
  70.8 0.1 fusion.45
  71.0 0.1 fusion.47
  71.1 0.1 fusion.49
  71.3 0.1 fusion.51
  71.4 0.1 fusion.53
  71.6 0.1 fusion.55
  72.6 14.7 %fusion.68 = f32[1024,1024]{1,0:T(8,128)} fusion(f32[1024,1024]{0,1:T(8,128)S(1)} %fusion.3), kind=kOutput, calls=%fused_computation.134 | convolution fusion | flops 12884901888 | bytes 8388608 | tf_op jit(solution)/shard_map/dot_general | solution.py:135
  87.4 266.6 %all-reduce.2.cloned.1.call-done.g_ref = f32[1024,1024]{1,0:T(8,128)} async-done(((f32[1024,1024]{1,0:T(8,128)}), f32[1024,1024]{1,0:T(8,128)}) %all-reduce.2.cloned.1.call-update) | async-done | bytes 4194320 | tf_op jit(solution)/shard_map/psum | solution.py:142
  354.1 2.2 copy-done
  356.2 49.8 %shard_map.37 = f32[1024,1024]{1,0:T(8,128)} custom-call(f32[1024,1024]{1,0:T(8,128)S(1)} %copy-done), custom_call_target="tpu_custom_call" | custom-call | tf_op jit(solution)/shard_map/pallas_call | solution.py:101
  (18 shorter events, 1.4 us)
Async XLA Ops:
  6.5 45.5 %copy-start.1 = (s32[8]{0:T(128)S(1)}, s32[8]{0:T(128)}, u32[]{:S(2)}) copy-start(s32[8]{0:T(128)} %param.5) | copy-start | bytes 100
  6.5 41.4 %reduce-scatter.2.cloned.1.call-start = ((), (), s32[]{:S(2)}) async-start(), calls=%async_computation.1 | async-start | bytes 2621440 | tf_op jit(solution)/shard_map/reduce_scatter | solution.py:122
  11.7 342.3 %all-reduce.2.cloned.1.call-start = ((), (), s32[]{:S(2)}) async-start(), calls=%async_computation.2 | async-start | bytes 8388608 | tf_op jit(solution)/shard_map/psum | solution.py:142
  49.1 18.7 %collective-permute-start = (f32[512,128]{0,1:T(8,128)S(1)}, f32[512,128]{0,1:T(8,128)S(1)}, u32[]{:S(2)}, u32[]{:S(2)}) collective-permute-start(f32[512,128]{0,1:T(8,128)S(1)} %slice.27), channel_id=1, source_target_pairs={{1,0},{2,1},{3,2},{4,3},{5,4},{6,5},{7,6},{8,7},{9,8},{10,9},{11,1... | collective-permute-start | bytes 786440 | tf_op jit(solution)/shard_map/ppermute | solution.py:123
  354.1 2.2 copy-start
Sparse Core Ops, SparseCore 0:
  11.8 36.0 reduce-scatter.1
  87.5 266.4 all-reduce.1

commit v2 on v1

v2 whole, which is shorter than its diff:
```python
import functools
import math

import jax
import jax.numpy as jnp
from jax import lax
from jax.experimental import pallas as pl
from jax.experimental.pallas import tpu as pltpu
from jax.sharding import PartitionSpec as P

NODES = 128
CH = 2048
MAXLAG = 512
F32 = jnp.float32
MESH = pl.DeviceIdType.MESH
VMEM = pl.BlockSpec(memory_space=pltpu.VMEM)
NB = 128


def first_block(i, count):
    return i * count - i * (i - 1) // 2


def gram_body(rows, lag_count, groups, lags_ref, ext_ref, out_ref, rot_ref, hi_ref, lo_ref):
    width = NODES // groups
    per_tile = NB // width
    count = lag_count * NODES // NB
    chunk = 128
    for r in range(1, per_tile):
        rot_ref[r - 1] = pltpu.roll(ext_ref[...], width * r, 1)
    place = lax.broadcasted_iota(jnp.int32, (chunk, NB), 1) // width
    for tile in range(count):
        group, half = tile // (count // groups), tile % (count // groups)

        def build(step, _):
            value = None
            for m in range(per_tile):
                first = lags_ref[half * per_tile + m] + step * chunk
                r = (m - group) % per_tile
                if r == 0:
                    piece = ext_ref[pl.ds(first, chunk), :]
                else:
                    piece = rot_ref[r - 1, pl.ds(first, chunk), :]
                value = piece if value is None else jnp.where(place == m, piece, value)
            high = value.astype(jnp.bfloat16)
            low = (value - high.astype(F32)).astype(jnp.bfloat16)
            at = pl.ds(pl.multiple_of(step * chunk, chunk), chunk)
            hi_ref[at, tile * NB : (tile + 1) * NB] = high
            lo_ref[at, tile * NB : (tile + 1) * NB] = low
            return 0

        lax.fori_loop(0, rows // chunk, build, 0)
    dims = (((0,), (0,)), ((), ()))
    for i in range(count):
        mine = slice(i * NB, (i + 1) * NB)
        rest = slice(i * NB, count * NB)
        a, b = hi_ref[:, mine], lo_ref[:, mine]
        value = lax.dot_general(a, lo_ref[:, rest], dims, preferred_element_type=F32)
        value += lax.dot_general(b, hi_ref[:, rest], dims, preferred_element_type=F32)
        value += lax.dot_general(a, hi_ref[:, rest], dims, preferred_element_type=F32)
        for j in range(i, count):
            out_ref[first_block(i, count) + j - i] = value[:, (j - i) * NB : (j - i + 1) * NB]


def local_gram(lags, extended, rows, groups):
    lag_count = lags.shape[0]
    size = lag_count * NODES
    count = size // NB
    return pl.pallas_call(
        functools.partial(gram_body, rows, lag_count, groups),
        out_shape=jax.ShapeDtypeStruct((count * (count + 1) // 2, NB, NB), F32),
        in_specs=[pl.BlockSpec(memory_space=pltpu.SMEM), VMEM],
        out_specs=VMEM,
        scratch_shapes=[
            pltpu.VMEM((NB // (NODES // groups) - 1,) + extended.shape, F32),
            pltpu.VMEM((rows, size), jnp.bfloat16),
            pltpu.VMEM((rows, size), jnp.bfloat16),
        ],
        compiler_params=pltpu.CompilerParams(vmem_limit_bytes=48 << 20),
    )(lags, extended)


NX, NY, NZ = 4, 4, 8


def place():
    x = lax.axis_index("chan")
    t = lax.axis_index("tm")
    return x, t // (NZ * 2), lax.rem(t // 2, NZ), lax.rem(t, 2)


def device(x, y, z, c):
    return {"tm": (y * NZ + z) * 2 + c, "chan": x}


def remote(src, dst, send, recv, target):
    return pltpu.make_async_remote_copy(
        src_ref=src, dst_ref=dst, send_sem=send, recv_sem=recv,
        device_id=target, device_id_type=MESH,
    )


def sum_body(half, x_ref, out_ref, rc, h, ra, sa, rb, y18, rz, send, recv):
    x, y, z, c = place()
    quarter = half // 2 // 4
    small = quarter // 4
    piece = 2 * small // 6
    barrier = pltpu.get_barrier_semaphore()
    near = [device(x, y, z, 1 - c)]
    near += [device(lax.rem(x + d, NX), y, z, c) for d in range(1, NX)]
    near += [device(x, lax.rem(y + d, NY), z, c) for d in range(1, NY)]
    near += [device(x, y, lax.rem(z + d, NZ), c) for d in range(1, NZ)]
    for dev in near:
        pl.semaphore_signal(barrier, inc=1, device_id=dev, device_id_type=MESH)
    pl.semaphore_wait(barrier, len(near))
    sem = iter(range(64))

    def ring(color, d, first):
        along_x = (color == 0) == first
        if along_x:
            at = lax.rem(x + d, NX)
            return device(at, y, z, c), at
        at = lax.rem(y + d, NY)
        return device(x, at, z, c), at

    work = []
    for color in range(2):
        s = next(sem)
        lo = color * half // 2
        cp = remote(x_ref.at[pl.ds((1 - c) * half + lo, half // 2)], rc.at[pl.ds(lo, half // 2)],
                    send.at[s], recv.at[s], device(x, y, z, 1 - c))
        cp.start()
        work.append(cp)
    for color in range(2):
        work[color].wait_recv()
        lo = color * half // 2
        h[lo : lo + half // 2] = x_ref[pl.ds(c * half + lo, half // 2)] + rc[lo : lo + half // 2]
        for d in range(1, 4):
            s = next(sem)
            dev, at = ring(color, d, True)
            cp = remote(h.at[pl.ds(lo + at * quarter, quarter)], ra.at[color, d - 1],
                        send.at[s], recv.at[s], dev)
            cp.start()
            work.append(cp)
    for color in range(2):
        mine = work[2 + 3 * color : 5 + 3 * color]
        for cp in mine:
            cp.wait_recv()
        _, at = ring(color, 0, True)
        lo = color * half // 2
        sa[color] = ((h[pl.ds(lo + at * quarter, quarter)] + ra[color, 0])
                     + (ra[color, 1] + ra[color, 2]))
        for d in range(1, 4):
            s = next(sem)
            dev, at = ring(color, d, False)
            cp = remote(sa.at[color, pl.ds(at * small, small)], rb.at[color, d - 1],
                        send.at[s], recv.at[s], dev)
            cp.start()
            work.append(cp)
    for color in range(2):
        mine = work[8 + 3 * color : 11 + 3 * color]
        for cp in mine:
            cp.wait_recv()
        _, at = ring(color, 0, False)
        y18[color * small : (color + 1) * small] = (
            (sa[color, pl.ds(at * small, small)] + rb[color, 0]) + (rb[color, 1] + rb[color, 2]))
    for cp in work:
        cp.wait_send()
    zcopies = []
    for d in range(1, NZ):
        s = next(sem)
        to = lax.rem(z + d, NZ)
        own = jnp.minimum(to, 5)
        cp = remote(y18.at[pl.ds(own * piece, piece)], rz.at[d - 1], send.at[s], recv.at[s],
                    device(x, y, to, c))
        pl.when(to < 6)(cp.start)
        zcopies.append((cp, to))
    base = c * half

    def spot(p):
        color = p // 3
        chunk = jnp.where(color == 0, x * 4 + y, y * 4 + x)
        return base + color * (half // 2) + chunk * small + lax.rem(p, 3) * piece

    own = jnp.minimum(z, 5)

    @pl.when(z < 6)
    def _():
        total = y18[pl.ds(own * piece, piece)]
        for d in range(1, NZ):
            zcopies[d - 1][0].wait_recv()
            total = total + rz[d - 1]
        out_ref[pl.ds(spot(own), piece)] = total

    back = []
    for d in range(1, NZ):
        s = next(sem)
        to = lax.rem(z + d, NZ)
        at = pl.ds(spot(own), piece)
        cp = remote(out_ref.at[at], out_ref.at[at], send.at[s], recv.at[s], device(x, y, to, c))
        pl.when(z < 6)(cp.start)
        back.append(cp)
    for d in range(1, NZ):
        source = lax.rem(z - d + NZ, NZ)
        pl.when(source < 6)(back[d - 1].wait_recv)
    work = []
    for color in range(2):
        _, mine = ring(color, 0, True)
        _, sub = ring(color, 0, False)
        at = pl.ds(base + color * (half // 2) + mine * quarter + sub * small, small)
        for d in range(1, 4):
            s = next(sem)
            dev, _ = ring(color, d, False)
            cp = remote(out_ref.at[at], out_ref.at[at], send.at[s], recv.at[s], dev)
            cp.start()
            work.append(cp)
    for color in range(2):
        for cp in work[3 * color : 3 * color + 3]:
            cp.wait_recv()
        _, mine = ring(color, 0, True)
        at = pl.ds(base + color * (half // 2) + mine * quarter, quarter)
        for d in range(1, 4):
            s = next(sem)
            dev, _ = ring(color, d, True)
            cp = remote(out_ref.at[at], out_ref.at[at], send.at[s], recv.at[s], dev)
            cp.start()
            work.append(cp)
    for color in range(2):
        for cp in work[6 + 3 * color : 9 + 3 * color]:
            cp.wait_recv()
        s = next(sem)
        at = pl.ds(base + color * (half // 2), half // 2)
        cp = remote(out_ref.at[at], out_ref.at[at], send.at[s], recv.at[s], device(x, y, z, 1 - c))
        cp.start()
        work.append(cp)
    for cp in work[12:]:
        cp.wait_recv()
    for cp in work:
        cp.wait_send()
    for cp, to in zcopies:
        pl.when(to < 6)(cp.wait_send)
    for cp in back:
        pl.when(z < 6)(cp.wait_send)


def sum_all(value):
    units = value.shape[0]
    half = units // 2
    quarter = half // 8
    small = quarter // 4
    piece = 2 * small // 6
    tile = value.shape[1:]
    buf = lambda *lead: pltpu.VMEM(lead + tile, F32)
    return pl.pallas_call(
        functools.partial(sum_body, half),
        out_shape=jax.ShapeDtypeStruct(value.shape, F32),
        in_specs=[VMEM],
        out_specs=VMEM,
        scratch_shapes=[
            buf(half), buf(half), buf(2, 3, quarter), buf(2, quarter), buf(2, 3, small),
            buf(2 * small), buf(7, piece),
            pltpu.SemaphoreType.DMA((64,)), pltpu.SemaphoreType.DMA((64,)),
        ],
        compiler_params=pltpu.CompilerParams(
            collective_id=1, has_side_effects=True, vmem_limit_bytes=48 << 20),
    )(value)

def lanes(x, c):
    return jnp.broadcast_to(x[:, c : c + 1], x.shape)


def subs(x, r):
    return jnp.broadcast_to(x[r : r + 1, :], x.shape)


def factor_block(rows):
    count = NB // 8
    lane = lax.broadcasted_iota(jnp.int32, (8, NB), 1)
    sub = lax.broadcasted_iota(jnp.int32, (8, NB), 0)
    rows = list(rows)
    inv = [jnp.where(lane == sub + 8 * i, 1.0, 0.0).astype(F32) for i in range(count)]
    for p in range(count):
        r0 = 8 * p
        col = [[None] * count for _ in range(8)]
        for j in range(8):
            for b in range(p, count):
                col[j][b] = lanes(rows[b], r0 + j)
        e = [[None] * 8 for _ in range(8)]
        for i in range(8):
            for j in range(i, 8):
                e[i][j] = subs(col[i][p], j)
        rinv = [None] * 8
        for j in range(8):
            rinv[j] = 1.0 / e[j][j]
            for i in range(j + 1, 8):
                for k in range(i, 8):
                    e[i][k] = e[i][k] - (e[j][i] * e[j][k]) * rinv[j]
        diag = e[7][7]
        for j in range(7):
            diag = jnp.where(sub == j, e[j][j], diag)
        rs = lax.rsqrt(diag)
        for b in range(p, count):
            for j in range(8):
                v = col[j][b]
                for i in range(j):
                    v = v - col[i][b] * e[i][j]
                v = v * rinv[j]
                if b == p:
                    v = jnp.where(sub > j, v, 0.0)
                col[j][b] = v
        for j in range(8):
            ra, rw = subs(rows[p], j), subs(inv[p], j)
            for b in range(p, count):
                rows[b] = rows[b] - col[j][b] * ra
                inv[b] = inv[b] - col[j][b] * rw
        rows[p] = jnp.where(lane >= sub + r0, rows[p] * rs, 0.0)
        inv[p] = inv[p] * rs
    return rows, inv


DOT = dict(precision=lax.Precision.HIGHEST, preferred_element_type=F32)


def factor_body(count, scale, g_ref, r_ref, w_ref, d_ref):
    r_ref[...] = jnp.zeros_like(r_ref)

    def update(k):
        r0 = k * NB
        first = first_block(k, count)
        for j in range(k, count):
            r_ref[r0 : r0 + NB, j * NB : (j + 1) * NB] = g_ref[first + j - k] * scale
        if k > 0:
            r_ref[r0 : r0 + NB, r0:] -= lax.dot_general(
                r_ref[0:r0, r0 : r0 + NB], r_ref[0:r0, r0:], (((0,), (0,)), ((), ())), **DOT
            )
        d_ref[...] = r_ref[r0 : r0 + NB, r0 : r0 + NB]

    def panel(k):
        r0 = k * NB
        r_ref[r0 : r0 + NB, r0 : r0 + NB] = d_ref[...]
        if k + 1 < count:
            r_ref[r0 : r0 + NB, r0 + NB :] = lax.dot_general(
                w_ref[...], r_ref[r0 : r0 + NB, r0 + NB :], (((1,), (0,)), ((), ())), **DOT
            )

    def step(k, _):
        lax.switch(k, [functools.partial(update, i) for i in range(count)])
        rows, inv = factor_block([d_ref[8 * i : 8 * i + 8, :] for i in range(NB // 8)])
        for i in range(NB // 8):
            d_ref[8 * i : 8 * i + 8, :] = rows[i]
            w_ref[8 * i : 8 * i + 8, :] = inv[i]
        lax.switch(k, [functools.partial(panel, i) for i in range(count)])
        return 0

    lax.fori_loop(0, count, step, 0)


def upper_factor(blocks, count, scale):
    size = count * NB
    return pl.pallas_call(
        functools.partial(factor_body, count, scale),
        out_shape=jax.ShapeDtypeStruct((size, size), F32),
        in_specs=[VMEM],
        out_specs=VMEM,
        scratch_shapes=[pltpu.VMEM((NB, NB), F32)] * 2,
        compiler_params=pltpu.CompilerParams(vmem_limit_bytes=48 << 20),
    )(blocks)

def on_device(signals, channel_node, lag_offsets):
    axes = ("tm", "chan")
    parts = lax.axis_size("tm") * lax.axis_size("chan")
    groups = lax.axis_size("chan")
    count = lag_offsets.shape[0] * NODES // NB
    node_scale = 1.0 / math.sqrt(CH // NODES)
    onehot = (channel_node[:, None] == jnp.arange(NODES, dtype=jnp.int32)[None, :]).astype(
        jnp.bfloat16
    )
    partial_sum = jnp.dot(signals, onehot, preferred_element_type=jnp.float32)
    node_rows = lax.psum_scatter(partial_sum, "chan", scatter_dimension=0, tiled=True) * node_scale
    halo = lax.ppermute(node_rows[:MAXLAG], axes, [(i, i - 1) for i in range(1, parts)])
    extended = jnp.concatenate([node_rows, halo], axis=0)
    rows = node_rows.shape[0]
    blocks = local_gram(lag_offsets, extended, rows, groups)
    total = sum_all(blocks.reshape(-1, 8, NB)).reshape(blocks.shape)
    return upper_factor(total, count, 1.0 / (rows * parts))


def solution(mesh):
    in_specs = (P("tm", "chan"), P("chan"), P())
    out_specs = P()
    return jax.shard_map(
        on_device, mesh=mesh, in_specs=in_specs, out_specs=out_specs, check_vma=False
    )
```

time: 414 us -> 170 us (0.41)
  waiting for transfers between devices: 303 us -> 42.4 us
  Pallas kernels: 49.8 us -> 105 us
  between operations: 28.7 us -> 13.4 us
  matrix products: 19.9 us -> 4.87 us
  other arithmetic: 5.69 us -> 1.13 us
    psum x1 -> x0, waiting for transfers between devices: 267 us -> none  [on_device(): gram = lax.psum(local_gram, axes)]
    pallas_call x1 -> x3, Pallas kernels: 49.8 us -> 105 us  [the longest x1 49.7 us: upper_factor(): pl.pallas_call(functools.partial(factor_body, count, scale), out_shape=ja...]
    dot_general x1 -> x0, matrix products: 14.7 us -> none  [on_device(): lax.dot_general(hankel, hankel, (((0,), (0,)), ((), ())), precision=lax.P...]
    ppermute x1, waiting for transfers between devices: 0.01 us -> 6.16 us  [on_device(): lax.ppermute(node_rows[:MAXLAG], axes, [(i, i - 1) for i in range(1, part...]
    unnamed x31 -> x0, other arithmetic: 4.47 us -> none
  transfers between devices with their start and end apart: 3 -> 2, of which waited for: 2 -> 2; matrix products, arithmetic and copies ran while one was open for 0% -> 0% of each run, Pallas kernels for 0% -> 0%
where the time goes in v2:
time: 170 us
  Pallas kernels  105 us (62%)
  waiting for transfers between devices  42.4 us (25%)
  between operations  13.4 us (8%)
  matrix products  4.87 us (3%)
  starting transfers between devices  2.97 us (2%)
    pallas_call x1, Pallas kernels, upper_factor(): pl.pallas_call(functools.partial(factor_body, count, scale), out_shape=ja...  49.7 us
    pallas_call x1, Pallas kernels, sum_all(): pl.pallas_call(functools.partial(sum_body, half), out_shape=jax.ShapeDtyp...  47.9 us
    reduce_scatter x1, waiting for transfers between devices, on_device(): lax.psum_scatter(partial_sum, 'chan', scatter_dimension=0, tiled=True)  36.2 us
    pallas_call x1, Pallas kernels, local_gram(): pl.pallas_call(functools.partial(gram_body, rows, lag_count, groups), out...  7.42 us
    ppermute x1, waiting for transfers between devices, on_device(): lax.ppermute(node_rows[:MAXLAG], axes, [(i, i - 1) for i in range(1, part...  6.16 us
    dot_general x1, matrix products, on_device(): partial_sum = jnp.dot(signals, onehot, preferred_element_type=jnp.float32)  4.87 us
  transfers between devices with their start and end apart: 2, of which 2 were waited for; matrix products, arithmetic and copies ran while one was open for 0% of the time, Pallas kernels for 0%

profile of v2, /device:TPU:1, one launch (start us, length us, event | category | flops | bytes accessed | tf_op | source)
XLA Modules:
  0.0 169.8 jit_solution(15613432998761702849)
XLA Ops:
  6.5 0.0 reduce-scatter.2.cloned.1.call-start
  6.5 4.9 %convolution_bitcast_fusion = f32[4096,128]{1,0:T(8,128)} fusion(bf16[4096,512]{1,0:T(8,128)(2,1)} %param.3, s32[512]{0:T(512)} %param.4), kind=kOutput, calls=%fused_computation | convolution fusion | flops 536936448 | bytes 6293504 | tf_op jit(solution)/shard_map/dot_general | solution.py:378
  11.4 0.0 copy-start
  11.4 0.0 reduce-scatter.2.cloned.1.call-update
  11.4 36.2 %reduce-scatter.2.cloned.1.call-done = f32[1024,128]{1,0:T(8,128)} async-done(((f32[4096,128]{1,0:T(8,128)}), f32[1024,128]{1,0:T(8,128)}) %reduce-scatter.2.cloned.1.call-update) | async-done | bytes 524304 | tf_op jit(solution)/shard_map/reduce_scatter | solution.py:379
  47.7 1.1 broadcast_multiply_fusion
  48.8 3.0 %collective-permute-start = (f32[512,128]{1,0:T(8,128)S(1)}, f32[512,128]{1,0:T(8,128)S(1)}, u32[]{:S(2)}, u32[]{:S(2)}) collective-permute-start(f32[512,128]{1,0:T(8,128)S(1)} %slice.4), channel_id=1, source_target_pairs={{1,0},{2,1},{3,2},{4,3},{5,4},{6,5},{7,6},{8,7},{9,8},{10,9},{11,1... | collective-permute-start | bytes 786440 | tf_op jit(solution)/shard_map/ppermute | solution.py:380
  51.7 6.2 %collective-permute-done = f32[512,128]{1,0:T(8,128)S(1)} collective-permute-done((f32[512,128]{1,0:T(8,128)S(1)}, f32[512,128]{1,0:T(8,128)S(1)}, u32[]{:S(2)}, u32[]{:S(2)}) %collective-permute-start) | collective-permute-done | bytes 262176 | tf_op jit(solution)/shard_map/ppermute | solution.py:380
  57.9 0.1 pad_maximum_fusion.ext_ref
  58.0 0.0 copy-done
  58.0 7.4 %shard_map.37 = f32[36,128,128]{2,1,0:T(8,128)S(1)} custom-call(s32[8]{0:T(128)S(1)} %copy-done, f32[1536,128]{1,0:T(8,128)S(1)} %pad_maximum_fusion.ext_ref), custom_call_target="tpu_custom_call" | custom-call | tf_op jit(solution)/shard_map/pallas_call | solution.py:69
  65.4 47.9 %shard_map.38 = f32[576,8,128]{2,1,0:T(8,128)S(1)} custom-call(f32[576,8,128]{2,1,0:T(8,128)S(1)} %bitcast.6), custom_call_target="tpu_custom_call" | custom-call | tf_op jit(solution)/shard_map/pallas_call | solution.py:254
  113.3 49.7 %shard_map.39 = f32[1024,1024]{1,0:T(8,128)} custom-call(f32[36,128,128]{2,1,0:T(8,128)S(1)} %bitcast.5), custom_call_target="tpu_custom_call" | custom-call | tf_op jit(solution)/shard_map/pallas_call | solution.py:360
  (1 shorter events, 0.0 us)
Async XLA Ops:
  6.5 41.1 %reduce-scatter.2.cloned.1.call-start = ((), (), s32[]{:S(2)}) async-start(), calls=%async_computation.1 | async-start | bytes 2621440 | tf_op jit(solution)/shard_map/reduce_scatter | solution.py:379
  11.4 46.6 %copy-start = (s32[8]{0:T(128)S(1)}, s32[8]{0:T(128)}, u32[]{:S(2)}) copy-start(s32[8]{0:T(128)} %lags_ref.1) | copy-start | bytes 100
  48.8 9.1 %collective-permute-start = (f32[512,128]{1,0:T(8,128)S(1)}, f32[512,128]{1,0:T(8,128)S(1)}, u32[]{:S(2)}, u32[]{:S(2)}) collective-permute-start(f32[512,128]{1,0:T(8,128)S(1)} %slice.4), channel_id=1, source_target_pairs={{1,0},{2,1},{3,2},{4,3},{5,4},{6,5},{7,6},{8,7},{9,8},{10,9},{11,1... | collective-permute-start | bytes 786440 | tf_op jit(solution)/shard_map/ppermute | solution.py:380
Sparse Core Ops, SparseCore 0:
  11.6 36.0 reduce-scatter.1

commit v3 on v2

--- a/solution.py
+++ b/solution.py
@@ -264,6 +264,141 @@
         compiler_params=pltpu.CompilerParams(
             collective_id=1, has_side_effects=True, vmem_limit_bytes=48 << 20),
     )(value)
+
+def node_body(s_hbm, node_ref, ext_ref, sig, part, far, near, pair, fwd, load, send, recv):
+    x, y, z, c = place()
+    t = lax.axis_index("tm")
+    rows = part.shape[0] // 4
+    half, quarter = rows // 2, rows // 4
+
+    def chunk_of(at):
+        return jnp.where(c == 0, at, 3 - at)
+
+    flip = (lambda v: v + 1 - 2 * lax.rem(v, 2), lambda v: 3 - v)
+    others = (flip[0](x), flip[1](x))
+    opposite = lax.rem(x + 2, 4)
+    order = (opposite, others[0], others[1], x)
+    loads = []
+    for ph in range(2):
+        for i, at in enumerate(order):
+            rows_at = pl.ds(pl.multiple_of(chunk_of(at) * rows + ph * half, half), half)
+            cp = pltpu.make_async_copy(s_hbm.at[rows_at], sig.at[rows_at], load.at[ph * 4 + i])
+            cp.start()
+            loads.append((cp, rows_at))
+    b = chunk_of(x)
+    has_to = jnp.logical_or(b > 0, t > 0)
+    has_from = jnp.logical_or(b < 3, t < 2 * NY * NZ - 1)
+    step = 1 - 2 * c
+    to = {"tm": jnp.where(b > 0, t, jnp.maximum(t - 1, 0)), "chan": jnp.where(b > 0, x - step, x)}
+    source = {"tm": jnp.where(b < 3, t, jnp.minimum(t + 1, 2 * NY * NZ - 1)),
+              "chan": jnp.where(b < 3, x + step, x)}
+    barrier = pltpu.get_barrier_semaphore()
+    link = tuple(device(at, y, z, c) for at in others)
+    for dev in link:
+        pl.semaphore_signal(barrier, inc=1, device_id=dev, device_id_type=MESH)
+
+    @pl.when(has_to)
+    def _():
+        pl.semaphore_signal(barrier, inc=1, device_id=to, device_id_type=MESH)
+
+    @pl.when(has_from)
+    def _():
+        pl.semaphore_signal(barrier, inc=1, device_id=source, device_id_type=MESH)
+
+    scale = 1.0 / math.sqrt(CH // NODES)
+    chans = node_ref.shape[1]
+    match = lax.broadcasted_iota(jnp.int32, (NODES, chans), 0) == node_ref[...]
+    onehot = jnp.where(match, scale, 0.0).astype(jnp.bfloat16)
+
+    def sums(ph, i):
+        cp, rows_at = loads[ph * 4 + i]
+        cp.wait()
+        part[rows_at] = lax.dot_general(sig[rows_at], onehot, (((1,), (1,)), ((), ())),
+                                        preferred_element_type=F32)
+
+    def piece(at, ph, color):
+        return pl.ds(pl.multiple_of(chunk_of(at) * rows + ph * half + color * quarter, quarter), quarter)
+
+    def copy(src, dst, kind, ph, color, dev):
+        s = (kind * 2 + ph) * 2 + color
+        return remote(src, dst, send.at[s], recv.at[s], dev)
+
+    def fars(ph):
+        return [copy(part.at[piece(opposite, ph, k)], far.at[ph, k], 0, ph, k, link[k]) for k in range(2)]
+
+    def nears(ph):
+        return [copy(part.at[piece(others[k], ph, k)], near.at[ph, k], 1, ph, k, link[k]) for k in range(2)]
+
+    def forwards(ph):
+        return [copy(fwd.at[ph, k], pair.at[ph, k], 2, ph, k, link[1 - k]) for k in range(2)]
+
+    sums(0, 0)
+    count = 2 + has_to.astype(jnp.int32) + has_from.astype(jnp.int32)
+    pl.semaphore_wait(barrier, count)
+    work = [fars(0), nears(0), forwards(0), fars(1), nears(1), forwards(1)]
+
+    def forward(ph):
+        for k in range(2):
+            work[3 * ph][k].wait_recv()
+            fwd[ph, k] = part[piece(others[1 - k], ph, k)] + far[ph, k]
+            work[3 * ph + 2][k].start()
+
+    def finish(ph):
+        for k in range(2):
+            work[3 * ph + 1][k].wait_recv()
+            work[3 * ph + 2][k].wait_recv()
+            at = ph * half + k * quarter
+            ext_ref[at : at + quarter] = part[piece(x, ph, k)] + near[ph, k] + pair[ph, k]
+
+    for cp in work[0]:
+        cp.start()
+    sums(0, 1)
+    work[1][0].start()
+    sums(0, 2)
+    work[1][1].start()
+    for i in range(4):
+        sums(1, i)
+    sums(0, 3)
+    forward(0)
+    for cp in work[3] + work[4]:
+        cp.start()
+    finish(0)
+    forward(1)
+    halo = remote(ext_ref.at[0:half], ext_ref.at[rows : rows + half], send.at[12], recv.at[12], to)
+    pl.when(has_to)(halo.start)
+
+    @pl.when(jnp.logical_not(has_from))
+    def _():
+        ext_ref[rows : rows + half] = jnp.zeros((half, NODES), F32)
+
+    finish(1)
+    pl.when(has_from)(halo.wait_recv)
+    for pair_of in work:
+        for cp in pair_of:
+            cp.wait_send()
+    pl.when(has_to)(halo.wait_send)
+
+
+def node_rows(signals, channel_node):
+    length, chans = signals.shape
+    rows = length // 4
+    quarter = rows // 4
+    buf = lambda: pltpu.VMEM((2, 2, quarter, NODES), F32)
+    return pl.pallas_call(
+        node_body,
+        out_shape=jax.ShapeDtypeStruct((rows + MAXLAG, NODES), F32),
+        in_specs=[pl.BlockSpec(memory_space=pl.ANY), VMEM],
+        out_specs=VMEM,
+        scratch_shapes=[
+            pltpu.VMEM((length, chans), jnp.bfloat16), pltpu.VMEM((length, NODES), F32),
+            buf(), buf(), buf(), buf(),
+            pltpu.SemaphoreType.DMA((8,)), pltpu.SemaphoreType.DMA((13,)),
+            pltpu.SemaphoreType.DMA((13,)),
+        ],
+        compiler_params=pltpu.CompilerParams(
+            collective_id=2, has_side_effects=True, vmem_limit_bytes=48 << 20),
+    )(signals, channel_node.reshape(1, chans))
+
 
 def lanes(x, c):
     return jnp.broadcast_to(x[:, c : c + 1], x.shape)
@@ -367,19 +502,11 @@
     )(blocks)
 
 def on_device(signals, channel_node, lag_offsets):
-    axes = ("tm", "chan")
     parts = lax.axis_size("tm") * lax.axis_size("chan")
     groups = lax.axis_size("chan")
     count = lag_offsets.shape[0] * NODES // NB
-    node_scale = 1.0 / math.sqrt(CH // NODES)
-    onehot = (channel_node[:, None] == jnp.arange(NODES, dtype=jnp.int32)[None, :]).astype(
-        jnp.bfloat16
-    )
-    partial_sum = jnp.dot(signals, onehot, preferred_element_type=jnp.float32)
-    node_rows = lax.psum_scatter(partial_sum, "chan", scatter_dimension=0, tiled=True) * node_scale
-    halo = lax.ppermute(node_rows[:MAXLAG], axes, [(i, i - 1) for i in range(1, parts)])
-    extended = jnp.concatenate([node_rows, halo], axis=0)
-    rows = node_rows.shape[0]
+    rows = signals.shape[0] // groups
+    extended = node_rows(signals, channel_node)
     blocks = local_gram(lag_offsets, extended, rows, groups)
     total = sum_all(blocks.reshape(-1, 8, NB)).reshape(blocks.shape)
     return upper_factor(total, count, 1.0 / (rows * parts))

time: 170 us -> 136 us (0.80)
  waiting for transfers between devices: 42.4 us -> 0 us
  Pallas kernels: 105 us -> 133 us
  between operations: 13.4 us -> 0.03 us
  matrix products: 4.87 us -> 0 us
  starting transfers between devices: 2.97 us -> 0 us
  local copies, waits for them, and re-layouts: 0.02 us -> 2.89 us
    reduce_scatter x1 -> x0, waiting for transfers between devices: 36.2 us -> none  [on_device(): lax.psum_scatter(partial_sum, 'chan', scatter_dimension=0, tiled=True)]
    pallas_call x0 -> x1, Pallas kernels: none -> 24.4 us  [node_rows(): pl.pallas_call(node_body, out_shape=jax.ShapeDtypeStruct((rows + MAXLAG,...]
    ppermute x1 -> x0, waiting for transfers between devices: 6.16 us -> none  [on_device(): lax.ppermute(node_rows[:MAXLAG], axes, [(i, i - 1) for i in range(1, part...]
    dot_general x1 -> x0, matrix products: 4.87 us -> none  [on_device(): partial_sum = jnp.dot(signals, onehot, preferred_element_type=jnp.float32)]
    pallas_call x1, Pallas kernels: 47.9 us -> 51.3 us  [sum_all(): pl.pallas_call(functools.partial(sum_body, half), out_shape=jax.ShapeDtyp...]
    ppermute x1 -> x0, starting transfers between devices: 2.97 us -> none  [on_device(): lax.ppermute(node_rows[:MAXLAG], axes, [(i, i - 1) for i in range(1, part...]
    unnamed x2 -> x6, local copies, waits for them, and re-layouts: 0.01 us -> 2.89 us
  transfers between devices with their start and end apart: 2 -> 0, of which waited for: 2 -> 0; matrix products, arithmetic and copies ran while one was open for 0% -> 0% of each run, Pallas kernels for 0% -> 0%
where the time goes in v3:
time: 136 us
  Pallas kernels  133 us (98%)
  local copies, waits for them, and re-layouts  2.89 us (2%)
    pallas_call x1, Pallas kernels, sum_all(): pl.pallas_call(functools.partial(sum_body, half), out_shape=jax.ShapeDtyp...  51.3 us
    pallas_call x1, Pallas kernels, upper_factor(): pl.pallas_call(functools.partial(factor_body, count, scale), out_shape=ja...  49.6 us
    pallas_call x1, Pallas kernels, node_rows(): pl.pallas_call(node_body, out_shape=jax.ShapeDtypeStruct((rows + MAXLAG,...  24.4 us
    pallas_call x1, Pallas kernels, local_gram(): pl.pallas_call(functools.partial(gram_body, rows, lag_count, groups), out...  7.4 us
    unnamed x6, local copies, waits for them, and re-layouts  2.89 us

profile of v3, /device:TPU:1, one launch (start us, length us, event | category | flops | bytes accessed | tf_op | source)
XLA Modules:
  0.0 135.7 jit_solution(9763025550957070571)
XLA Ops:
  0.0 0.0 copy-start.2
  0.0 0.0 copy-start
  0.0 2.2 %copy-done = bf16[4096,512]{1,0:T(8,128)(2,1)S(1)} copy-done((bf16[4096,512]{1,0:T(8,128)(2,1)S(1)}, bf16[4096,512]{1,0:T(8,128)(2,1)}, u32[]{:S(2)}) %copy-start) | copy-done | bytes 4194328
  2.2 0.0 copy-start.1
  2.2 0.7 copy-done.1
  2.9 24.4 %shard_map.37.ext_ref = f32[1536,128]{1,0:T(8,128)S(1)} custom-call(bf16[4096,512]{1,0:T(8,128)(2,1)S(1)} %copy-done, s32[1,512]{1,0:T(1,128)S(1)} %bitcast.5), custom_call_target="tpu_custom_call" | custom-call | tf_op jit(solution)/shard_map/pallas_call | solution.py:387
  27.3 0.0 copy-done.2
  27.3 7.4 %shard_map.38 = f32[36,128,128]{2,1,0:T(8,128)S(1)} custom-call(s32[8]{0:T(128)S(1)} %copy-done.2, f32[1536,128]{1,0:T(8,128)S(1)} %shard_map.37.ext_ref), custom_call_target="tpu_custom_call" | custom-call | tf_op jit(solution)/shard_map/pallas_call | solution.py:69
  34.7 51.3 %shard_map.39 = f32[576,8,128]{2,1,0:T(8,128)S(1)} custom-call(f32[576,8,128]{2,1,0:T(8,128)S(1)} %bitcast.4), custom_call_target="tpu_custom_call" | custom-call | tf_op jit(solution)/shard_map/pallas_call | solution.py:254
  86.0 49.6 %shard_map.40 = f32[1024,1024]{1,0:T(8,128)} custom-call(f32[36,128,128]{2,1,0:T(8,128)S(1)} %bitcast.3), custom_call_target="tpu_custom_call" | custom-call | tf_op jit(solution)/shard_map/pallas_call | solution.py:495
Async XLA Ops:
  0.0 27.3 %copy-start.2 = (s32[8]{0:T(128)S(1)}, s32[8]{0:T(128)}, u32[]{:S(2)}) copy-start(s32[8]{0:T(128)} %lags_ref.1) | copy-start | bytes 100
  0.0 2.2 %copy-start = (bf16[4096,512]{1,0:T(8,128)(2,1)S(1)}, bf16[4096,512]{1,0:T(8,128)(2,1)}, u32[]{:S(2)}) copy-start(bf16[4096,512]{1,0:T(8,128)(2,1)} %s_hbm.1) | copy-start | bytes 12582916
  2.2 0.7 copy-start.1

commit v4 on v3

--- a/solution.py
+++ b/solution.py
@@ -413,44 +413,56 @@
     lane = lax.broadcasted_iota(jnp.int32, (8, NB), 1)
     sub = lax.broadcasted_iota(jnp.int32, (8, NB), 0)
     rows = list(rows)
-    inv = [jnp.where(lane == sub + 8 * i, 1.0, 0.0).astype(F32) for i in range(count)]
+    upper, inv = [], []
+    cur = [lanes(rows[0], j) for j in range(8)]
     for p in range(count):
         r0 = 8 * p
-        col = [[None] * count for _ in range(8)]
+        raw = {b: [lanes(rows[b], r0 + j) for j in range(8)] for b in range(p + 1, count)}
+        ahead = [lanes(rows[p + 1], r0 + 8 + j) for j in range(8)] if p + 1 < count else None
+        here = jnp.logical_and(lane >= r0, lane < r0 + 8)
+        top, low = rows[p], jnp.where(here, jnp.where(lane == sub + r0, 1.0, 0.0), rows[p])
+        for b in range(p + 1, count):
+            rows[b] = jnp.where(here, 0.0, rows[b])
+        v, m, s, rinv = list(cur), [None] * 8, [[None] * 8 for _ in range(8)], [None] * 8
+        diag = None
         for j in range(8):
-            for b in range(p, count):
-                col[j][b] = lanes(rows[b], r0 + j)
-        e = [[None] * 8 for _ in range(8)]
-        for i in range(8):
-            for j in range(i, 8):
-                e[i][j] = subs(col[i][p], j)
-        rinv = [None] * 8
+            diag = v[j] if diag is None else jnp.where(sub >= j, v[j], diag)
+            rinv[j] = 1.0 / subs(v[j], j)
+            whole = v[j] * rinv[j]
+            for k in range(j + 1, 8):
+                s[j][k] = subs(v[j], k)
+                if k == j + 1:
+                    v[k] = v[k] - (v[j] * s[j][k]) * rinv[j]
+                else:
+                    v[k] = v[k] - whole * s[j][k]
+            m[j] = jnp.where(sub > j, whole, 0.0)
+        rs = lax.rsqrt(diag)
+        ra = []
         for j in range(8):
-            rinv[j] = 1.0 / e[j][j]
-            for i in range(j + 1, 8):
-                for k in range(i, 8):
-                    e[i][k] = e[i][k] - (e[j][i] * e[j][k]) * rinv[j]
-        diag = e[7][7]
-        for j in range(7):
-            diag = jnp.where(sub == j, e[j][j], diag)
-        rs = lax.rsqrt(diag)
-        for b in range(p, count):
+            ra.append(subs(low, j))
+            da = subs(top, j)
+            low = low - m[j] * ra[j]
+            top = top - m[j] * da
+        for b in range(p + 1, count):
+            u, mb = [], []
             for j in range(8):
-                v = col[j][b]
+                value = raw[b][j]
                 for i in range(j):
-                    v = v - col[i][b] * e[i][j]
-                v = v * rinv[j]
-                if b == p:
-                    v = jnp.where(sub > j, v, 0.0)
-                col[j][b] = v
-        for j in range(8):
-            ra, rw = subs(rows[p], j), subs(inv[p], j)
-            for b in range(p, count):
-                rows[b] = rows[b] - col[j][b] * ra
-                inv[b] = inv[b] - col[j][b] * rw
-        rows[p] = jnp.where(lane >= sub + r0, rows[p] * rs, 0.0)
-        inv[p] = inv[p] * rs
-    return rows, inv
+                    value = value - mb[i] * s[i][j]
+                u.append(value)
+                mb.append(value * rinv[j])
+            if b == p + 1:
+                cur = []
+                for i in range(8):
+                    value = ahead[i]
+                    for j in range(8):
+                        value = value - mb[j] * subs(u[j], i)
+                    cur.append(value)
+            for j in range(8):
+                rows[b] = rows[b] - mb[j] * ra[j]
+        upper.append(jnp.where(lane >= sub + r0, top * rs, 0.0))
+        inv.append(jnp.where(lane < r0 + 8, low * rs, 0.0))
+    return upper, inv
 
 
 DOT = dict(precision=lax.Precision.HIGHEST, preferred_element_type=F32)

time: 136 us -> 119 us (0.88)
  Pallas kernels: 133 us -> 116 us
    pallas_call x1, Pallas kernels: 49.6 us -> 33.2 us  [upper_factor(): pl.pallas_call(functools.partial(factor_body, count, scale), out_shape=ja...]
where the time goes in v4:
time: 119 us
  Pallas kernels  116 us (97%)
  local copies, waits for them, and re-layouts  2.89 us (2%)
    pallas_call x1, Pallas kernels, sum_all(): pl.pallas_call(functools.partial(sum_body, half), out_shape=jax.ShapeDtyp...  51.3 us
    pallas_call x1, Pallas kernels, upper_factor(): pl.pallas_call(functools.partial(factor_body, count, scale), out_shape=ja...  33.2 us
    pallas_call x1, Pallas kernels, node_rows(): pl.pallas_call(node_body, out_shape=jax.ShapeDtypeStruct((rows + MAXLAG,...  24.4 us
    pallas_call x1, Pallas kernels, local_gram(): pl.pallas_call(functools.partial(gram_body, rows, lag_count, groups), out...  7.42 us
    unnamed x6, local copies, waits for them, and re-layouts  2.89 us

profile of v4, /device:TPU:1, one launch (start us, length us, event | category | flops | bytes accessed | tf_op | source)
XLA Modules:
  0.0 119.3 jit_solution(10597620386289906153)
XLA Ops:
  0.0 0.0 copy-start.2
  0.0 0.0 copy-start
  0.0 2.2 %copy-done = bf16[4096,512]{1,0:T(8,128)(2,1)S(1)} copy-done((bf16[4096,512]{1,0:T(8,128)(2,1)S(1)}, bf16[4096,512]{1,0:T(8,128)(2,1)}, u32[]{:S(2)}) %copy-start) | copy-done | bytes 4194328
  2.2 0.0 copy-start.1
  2.2 0.7 copy-done.1
  2.9 24.4 %shard_map.37.ext_ref = f32[1536,128]{1,0:T(8,128)S(1)} custom-call(bf16[4096,512]{1,0:T(8,128)(2,1)S(1)} %copy-done, s32[1,512]{1,0:T(1,128)S(1)} %bitcast.5), custom_call_target="tpu_custom_call" | custom-call | tf_op jit(solution)/shard_map/pallas_call | solution.py:387
  27.3 0.0 copy-done.2
  27.3 7.4 %shard_map.38 = f32[36,128,128]{2,1,0:T(8,128)S(1)} custom-call(s32[8]{0:T(128)S(1)} %copy-done.2, f32[1536,128]{1,0:T(8,128)S(1)} %shard_map.37.ext_ref), custom_call_target="tpu_custom_call" | custom-call | tf_op jit(solution)/shard_map/pallas_call | solution.py:69
  34.8 51.3 %shard_map.39 = f32[576,8,128]{2,1,0:T(8,128)S(1)} custom-call(f32[576,8,128]{2,1,0:T(8,128)S(1)} %bitcast.4), custom_call_target="tpu_custom_call" | custom-call | tf_op jit(solution)/shard_map/pallas_call | solution.py:254
  86.0 33.2 %shard_map.40 = f32[1024,1024]{1,0:T(8,128)} custom-call(f32[36,128,128]{2,1,0:T(8,128)S(1)} %bitcast.3), custom_call_target="tpu_custom_call" | custom-call | tf_op jit(solution)/shard_map/pallas_call | solution.py:507
Async XLA Ops:
  0.0 27.3 %copy-start.2 = (s32[8]{0:T(128)S(1)}, s32[8]{0:T(128)}, u32[]{:S(2)}) copy-start(s32[8]{0:T(128)} %lags_ref.1) | copy-start | bytes 100
  0.0 2.2 %copy-start = (bf16[4096,512]{1,0:T(8,128)(2,1)S(1)}, bf16[4096,512]{1,0:T(8,128)(2,1)}, u32[]{:S(2)}) copy-start(bf16[4096,512]{1,0:T(8,128)(2,1)} %s_hbm.1) | copy-start | bytes 12582916
  2.2 0.7 copy-start.1

commit v5 on v0

v5 whole, which is shorter than its diff:
```python
import functools
import math

import jax
import jax.numpy as jnp
from jax import lax
from jax.experimental import pallas as pl
from jax.experimental.pallas import tpu as pltpu
from jax.sharding import PartitionSpec as P

NODES = 128
CH = 2048
MAXLAG = 512
F32 = jnp.float32
BF16 = jnp.bfloat16
MESH = pl.DeviceIdType.MESH
VMEM = pl.BlockSpec(memory_space=pltpu.VMEM)
NB = 128
NX, NY, NZ = 4, 4, 8
SEGMENTS = 3
OWNERS = 6


def first_block(i, count):
    return i * count - i * (i - 1) // 2


def device(x, y, z, c):
    return {"tm": (y * NZ + z) * 2 + c, "chan": x}


def remote(src, dst, send, recv, target):
    return pltpu.make_async_remote_copy(
        src_ref=src, dst_ref=dst, send_sem=send, recv_sem=recv,
        device_id=target, device_id_type=MESH,
    )


def gram_body(lag_count, lags_ref, s_hbm, node_ref, out_ref,
              sig, part, far, near, pair, fwd, own, land, rot, hi, lo,
              g, rc, h, ra, sa, rb, ys, rz, load, send, recv, ssend, srecv):
    x, t = lax.axis_index("chan"), lax.axis_index("tm")
    y, z, c = t // (NZ * 2), lax.rem(t // 2, NZ), lax.rem(t, 2)
    rows = own.shape[0]
    half, quarter = rows // 2, rows // 4

    def chunk_of(at):
        return jnp.where(c == 0, at, 3 - at)

    others = (x + 1 - 2 * lax.rem(x, 2), 3 - x)
    opposite = lax.rem(x + 2, 4)
    loads = []
    for ph in range(2):
        for i, at in enumerate((opposite, others[0], others[1], x)):
            rows_at = pl.ds(pl.multiple_of(chunk_of(at) * rows + ph * half, half), half)
            cp = pltpu.make_async_copy(s_hbm.at[rows_at], sig.at[rows_at], load.at[ph * 4 + i])
            cp.start()
            loads.append((cp, rows_at))
    b = chunk_of(x)
    has_to = jnp.logical_or(b > 0, t > 0)
    has_from = jnp.logical_or(b < 3, t < 2 * NY * NZ - 1)
    step = 1 - 2 * c
    to = {"tm": jnp.where(b > 0, t, jnp.maximum(t - 1, 0)), "chan": jnp.where(b > 0, x - step, x)}
    source = {"tm": jnp.where(b < 3, t, jnp.minimum(t + 1, 2 * NY * NZ - 1)),
              "chan": jnp.where(b < 3, x + step, x)}
    barrier = pltpu.get_barrier_semaphore()
    peers = [device(x, y, z, 1 - c)]
    peers += [device(lax.rem(x + d, NX), y, z, c) for d in range(1, NX)]
    peers += [device(x, lax.rem(y + d, NY), z, c) for d in range(1, NY)]
    peers += [device(x, y, lax.rem(z + d, NZ), c) for d in range(1, NZ)]
    for dev in peers:
        pl.semaphore_signal(barrier, inc=1, device_id=dev, device_id_type=MESH)

    @pl.when(has_to)
    def _():
        pl.semaphore_signal(barrier, inc=1, device_id=to, device_id_type=MESH)

    @pl.when(has_from)
    def _():
        pl.semaphore_signal(barrier, inc=1, device_id=source, device_id_type=MESH)

    scale = 1.0 / math.sqrt(CH // NODES)
    chans = node_ref.shape[1]
    match = lax.broadcasted_iota(jnp.int32, (NODES, chans), 0) == node_ref[...]
    onehot = jnp.where(match, scale, 0.0).astype(BF16)

    def sums(ph, i):
        cp, rows_at = loads[ph * 4 + i]
        cp.wait()
        part[rows_at] = lax.dot_general(sig[rows_at], onehot, (((1,), (1,)), ((), ())),
                                        preferred_element_type=F32)

    def piece(at, ph, color):
        first = chunk_of(at) * rows + ph * half + color * quarter
        return pl.ds(pl.multiple_of(first, quarter), quarter)

    link = tuple(device(at, y, z, c) for at in others)

    def copy(src, dst, kind, ph, color, dev):
        s = (kind * 2 + ph) * 2 + color
        return remote(src, dst, send.at[s], recv.at[s], dev)

    sums(0, 0)
    pl.semaphore_wait(barrier, len(peers) + has_to.astype(jnp.int32) + has_from.astype(jnp.int32))
    fars, nears, pairs = [], [], []
    for ph in range(2):
        fars.append([copy(part.at[piece(opposite, ph, k)], far.at[ph, k], 0, ph, k, link[k])
                     for k in range(2)])
        nears.append([copy(part.at[piece(others[k], ph, k)], near.at[ph, k], 1, ph, k, link[k])
                      for k in range(2)])
        pairs.append([copy(fwd.at[ph, k], pair.at[ph, k], 2, ph, k, link[1 - k])
                      for k in range(2)])

    def forward(ph):
        for k in range(2):
            fars[ph][k].wait_recv()
            fwd[ph, k] = part[piece(others[1 - k], ph, k)] + far[ph, k]
            pairs[ph][k].start()

    def finish(ph):
        for k in range(2):
            nears[ph][k].wait_recv()
            pairs[ph][k].wait_recv()
            at = ph * half + k * quarter
            own[at : at + quarter] = part[piece(x, ph, k)] + near[ph, k] + pair[ph, k]

    for cp in fars[0]:
        cp.start()
    sums(0, 1)
    nears[0][0].start()
    sums(0, 2)
    nears[0][1].start()
    for i in range(4):
        sums(1, i)
    sums(0, 3)
    forward(0)
    for cp in fars[1] + nears[1]:
        cp.start()
    finish(0)
    forward(1)
    halo = remote(own.at[0:half], land, send.at[12], recv.at[12], to)
    pl.when(has_to)(halo.start)
    finish(1)

    width = NODES // NX
    per_tile = NB // width
    count = lag_count * NODES // NB
    chunk = 128
    lane_group = lax.broadcasted_iota(jnp.int32, (chunk, NB), 1) // width

    def build(first_step, steps):
        for tile in range(count):
            group, top = tile // (count // NX), tile % (count // NX)

            def fill(i, _):
                value = None
                for m in range(per_tile):
                    first = lags_ref[top * per_tile + m] + i * chunk
                    got = rot[(m - group) % per_tile, pl.ds(first, chunk), :]
                    value = got if value is None else jnp.where(lane_group == m, got, value)
                high = value.astype(BF16)
                at = pl.ds(pl.multiple_of(i * chunk, chunk), chunk)
                hi[at, tile * NB : (tile + 1) * NB] = high
                lo[at, tile * NB : (tile + 1) * NB] = (value - high.astype(F32)).astype(BF16)
                return 0

            lax.fori_loop(first_step, first_step + steps, fill, 0)

    dims = (((0,), (0,)), ((), ()))

    def products(i, at, add):
        a, d = hi[at, i * NB : (i + 1) * NB], lo[at, i * NB : (i + 1) * NB]
        value = lax.dot_general(a, lo[at, i * NB :], dims, preferred_element_type=F32)
        value += lax.dot_general(d, hi[at, i * NB :], dims, preferred_element_type=F32)
        value += lax.dot_general(a, hi[at, i * NB :], dims, preferred_element_type=F32)
        for j in range(i, count):
            spot = 16 * (first_block(i, count) + j - i)
            block = value[:, (j - i) * NB : (j - i + 1) * NB].reshape(16, 8, NB)
            g[spot : spot + 16] = g[spot : spot + 16] + block if add else block

    for r in range(per_tile):
        rot[r, 0:rows] = own[...] if r == 0 else pltpu.roll(own[...], width * r, 1)
    steps = half // chunk
    build(0, steps)
    for i in range(count):
        products(i, slice(0, half), False)

    @pl.when(has_from)
    def _():
        halo.wait_recv()

    @pl.when(jnp.logical_not(has_from))
    def _():
        land[...] = jnp.zeros_like(land)

    for r in range(per_tile):
        rot[r, rows : rows + half] = land[...] if r == 0 else pltpu.roll(land[...], width * r, 1)
    build(steps, steps)

    units = g.shape[0] // SEGMENTS
    side = units // 2
    color_part = side // 2
    ring_part = color_part // 4
    small = ring_part // 4
    sems = iter(range(SEGMENTS * 42))
    ids = [[[next(sems) for _ in range(n)] for n in (2, 6, 6, 7, 7, 6, 6, 2)] for _ in range(SEGMENTS)]

    def ring(color, d, first):
        if (color == 0) == first:
            at = lax.rem(x + d, NX)
            return device(at, y, z, c), at
        at = lax.rem(y + d, NY)
        return device(x, at, z, c), at

    def send_to(src, dst, s, stage, n, dev):
        k = ids[s][stage][n]
        return remote(src, dst, ssend.at[k], srecv.at[k], dev)

    partner = device(x, y, z, 1 - c)
    plain = []
    stages = [[[] for _ in range(8)] for _ in range(SEGMENTS)]

    def go(s, stage, cp):
        cp.start()
        stages[s][stage].append(cp)
        plain.append(cp)

    def cores(s):
        for color in range(2):
            at = pl.ds(s * units + (1 - c) * side + color * color_part, color_part)
            go(s, 0, send_to(g.at[at], rc.at[s, color], s, 0, color, partner))

    def ring_first(s):
        for color in range(2):
            stages[s][0][color].wait_recv()
            at = pl.ds(s * units + c * side + color * color_part, color_part)
            h[s, color] = g[at] + rc[s, color]
            for d in range(1, 4):
                dev, spot = ring(color, d, True)
                go(s, 1, send_to(h.at[s, color, pl.ds(spot * ring_part, ring_part)],
                                 ra.at[s, color, d - 1], s, 1, 3 * color + d - 1, dev))

    def ring_second(s):
        for color in range(2):
            for cp in stages[s][1][3 * color : 3 * color + 3]:
                cp.wait_recv()
            _, spot = ring(color, 0, True)
            sa[s, color] = ((h[s, color, pl.ds(spot * ring_part, ring_part)] + ra[s, color, 0])
                            + (ra[s, color, 1] + ra[s, color, 2]))
            for d in range(1, 4):
                dev, spot = ring(color, d, False)
                go(s, 2, send_to(sa.at[s, color, pl.ds(spot * small, small)],
                                 rb.at[s, color, d - 1], s, 2, 3 * color + d - 1, dev))

    size = 2 * small // OWNERS
    mine = jnp.minimum(z, OWNERS - 1)

    def along_z(s):
        for color in range(2):
            for cp in stages[s][2][3 * color : 3 * color + 3]:
                cp.wait_recv()
            _, spot = ring(color, 0, False)
            ys[s, color * small : (color + 1) * small] = (
                (sa[s, color, pl.ds(spot * small, small)] + rb[s, color, 0])
                + (rb[s, color, 1] + rb[s, color, 2]))
        for d in range(1, NZ):
            dst = lax.rem(z + d, NZ)
            at = pl.ds(jnp.minimum(dst, OWNERS - 1) * size, size)
            cp = send_to(ys.at[s, at], rz.at[s, d - 1], s, 3, d - 1, device(x, y, dst, c))
            pl.when(dst < OWNERS)(cp.start)
            stages[s][3].append(cp)

    def spot_of(s, p):
        color = p // (OWNERS // 2)
        chunk_at = jnp.where(color == 0, x * 4 + y, y * 4 + x)
        return (s * units + c * side + color * color_part + chunk_at * small
                + lax.rem(p, OWNERS // 2) * size)

    def back_z(s):
        at = pl.ds(spot_of(s, mine), size)

        @pl.when(z < OWNERS)
        def _():
            total = ys[s, pl.ds(mine * size, size)]
            for d in range(1, NZ):
                stages[s][3][d - 1].wait_recv()
                total = total + rz[s, d - 1]
            out_ref[at] = total

        for d in range(1, NZ):
            cp = send_to(out_ref.at[at], out_ref.at[at], s, 4, d - 1,
                         device(x, y, lax.rem(z + d, NZ), c))
            pl.when(z < OWNERS)(cp.start)
            stages[s][4].append(cp)

    def back_second(s):
        for d in range(1, NZ):
            pl.when(lax.rem(z - d + NZ, NZ) < OWNERS)(stages[s][4][d - 1].wait_recv)
        for color in range(2):
            _, spot = ring(color, 0, True)
            _, sub = ring(color, 0, False)
            at = pl.ds(s * units + c * side + color * color_part + spot * ring_part + sub * small,
                       small)
            for d in range(1, 4):
                dev, _ = ring(color, d, False)
                go(s, 5, send_to(out_ref.at[at], out_ref.at[at], s, 5, 3 * color + d - 1, dev))

    def back_first(s):
        for color in range(2):
            for cp in stages[s][5][3 * color : 3 * color + 3]:
                cp.wait_recv()
            _, spot = ring(color, 0, True)
            at = pl.ds(s * units + c * side + color * color_part + spot * ring_part, ring_part)
            for d in range(1, 4):
                dev, _ = ring(color, d, True)
                go(s, 6, send_to(out_ref.at[at], out_ref.at[at], s, 6, 3 * color + d - 1, dev))

    def back_cores(s):
        for color in range(2):
            for cp in stages[s][6][3 * color : 3 * color + 3]:
                cp.wait_recv()
            at = pl.ds(s * units + c * side + color * color_part, color_part)
            go(s, 7, send_to(out_ref.at[at], out_ref.at[at], s, 7, color, partner))

    def last(s):
        for cp in stages[s][7]:
            cp.wait_recv()

    done = 0
    for s in range(SEGMENTS):
        while first_block(done, count) * 16 < (s + 1) * units:
            products(done, slice(half, rows), True)
            done += 1
        cores(s)
    chain = (ring_first, ring_second, along_z, back_z, back_second, back_first, back_cores, last)
    for slot in range(len(chain) + SEGMENTS - 1):
        for s in range(SEGMENTS):
            if 0 <= slot - s < len(chain):
                chain[slot - s](s)

    for ph in range(2):
        for cp in fars[ph] + nears[ph] + pairs[ph]:
            cp.wait_send()
    pl.when(has_to)(halo.wait_send)
    for cp in plain:
        cp.wait_send()
    for s in range(SEGMENTS):
        for d in range(1, NZ):
            pl.when(lax.rem(z + d, NZ) < OWNERS)(stages[s][3][d - 1].wait_send)
            pl.when(z < OWNERS)(stages[s][4][d - 1].wait_send)


def gram_blocks(signals, channel_node, lags):
    length, chans = signals.shape
    rows = length // NX
    size = lags.shape[0] * NODES
    count = size // NB
    blocks = count * (count + 1) // 2
    side = blocks * 16 // SEGMENTS // 2
    tiles = lambda *lead: pltpu.VMEM(lead + (8, NB), F32)
    quarters = pltpu.VMEM((2, 2, rows // 4, NODES), F32)
    S = SEGMENTS
    dma = pltpu.SemaphoreType.DMA
    total = pl.pallas_call(
        functools.partial(gram_body, lags.shape[0]),
        out_shape=jax.ShapeDtypeStruct((blocks * 16, 8, NB), F32),
        in_specs=[pl.BlockSpec(memory_space=pltpu.SMEM), pl.BlockSpec(memory_space=pl.ANY), VMEM],
        out_specs=VMEM,
        scratch_shapes=[
            pltpu.VMEM((length, chans), BF16), pltpu.VMEM((length, NODES), F32),
            quarters, quarters, quarters, quarters,
            pltpu.VMEM((rows, NODES), F32), pltpu.VMEM((MAXLAG, NODES), F32),
            pltpu.VMEM((NX, rows + MAXLAG, NODES), F32),
            pltpu.VMEM((rows, size), BF16), pltpu.VMEM((rows, size), BF16),
            tiles(blocks * 16), tiles(S, 2, side // 2), tiles(S, 2, side // 2),
            tiles(S, 2, 3, side // 8), tiles(S, 2, side // 8), tiles(S, 2, 3, side // 32),
            tiles(S, side // 16), tiles(S, NZ - 1, side // 16 // OWNERS),
            dma((8,)), dma((13,)), dma((13,)), dma((S * 42,)), dma((S * 42,)),
        ],
        compiler_params=pltpu.CompilerParams(
            collective_id=1, has_side_effects=True, vmem_limit_bytes=56 << 20),
    )(lags, signals, channel_node.reshape(1, chans))
    return total.reshape(blocks, NB, NB)


def lanes(x, c):
    return jnp.broadcast_to(x[:, c : c + 1], x.shape)


def subs(x, r):
    return jnp.broadcast_to(x[r : r + 1, :], x.shape)


def factor_block(rows):
    count = NB // 8
    lane = lax.broadcasted_iota(jnp.int32, (8, NB), 1)
    sub = lax.broadcasted_iota(jnp.int32, (8, NB), 0)
    rows = list(rows)
    upper, inv = [], []
    cur = [lanes(rows[0], j) for j in range(8)]
    for p in range(count):
        r0 = 8 * p
        raw = {b: [lanes(rows[b], r0 + j) for j in range(8)] for b in range(p + 1, count)}
        ahead = [lanes(rows[p + 1], r0 + 8 + j) for j in range(8)] if p + 1 < count else None
        here = jnp.logical_and(lane >= r0, lane < r0 + 8)
        top, low = rows[p], jnp.where(here, jnp.where(lane == sub + r0, 1.0, 0.0), rows[p])
        for b in range(p + 1, count):
            rows[b] = jnp.where(here, 0.0, rows[b])
        v, m, s, rinv = list(cur), [None] * 8, [[None] * 8 for _ in range(8)], [None] * 8
        diag = None
        for j in range(8):
            diag = v[j] if diag is None else jnp.where(sub >= j, v[j], diag)
            rinv[j] = 1.0 / subs(v[j], j)
            whole = v[j] * rinv[j]
            for k in range(j + 1, 8):
                s[j][k] = subs(v[j], k)
                if k == j + 1:
                    v[k] = v[k] - (v[j] * s[j][k]) * rinv[j]
                else:
                    v[k] = v[k] - whole * s[j][k]
            m[j] = jnp.where(sub > j, whole, 0.0)
        rs = lax.rsqrt(diag)
        ra = []
        for j in range(8):
            ra.append(subs(low, j))
            da = subs(top, j)
            low = low - m[j] * ra[j]
            top = top - m[j] * da
        for b in range(p + 1, count):
            u, mb = [], []
            for j in range(8):
                value = raw[b][j]
                for i in range(j):
                    value = value - mb[i] * s[i][j]
                u.append(value)
                mb.append(value * rinv[j])
            if b == p + 1:
                cur = []
                for i in range(8):
                    value = ahead[i]
                    for j in range(8):
                        value = value - mb[j] * subs(u[j], i)
                    cur.append(value)
            for j in range(8):
                rows[b] = rows[b] - mb[j] * ra[j]
        upper.append(jnp.where(lane >= sub + r0, top * rs, 0.0))
        inv.append(jnp.where(lane < r0 + 8, low * rs, 0.0))
    return upper, inv


DOT = dict(precision=lax.Precision.HIGHEST, preferred_element_type=F32)


def factor_body(count, scale, g_hbm, out_hbm, g_ref, r_ref, w_ref, d_ref, sem):
    def fetch(k):
        at = pl.ds(first_block(k, count), count - k)
        return pltpu.make_async_copy(g_hbm.at[at], g_ref.at[at], sem.at[count + k])

    for k in range(count):
        fetch(k).start()
    r_ref[...] = jnp.zeros_like(r_ref)

    def leave(k):
        at = pl.ds(k * NB, NB)
        return pltpu.make_async_copy(r_ref.at[at], out_hbm.at[at], sem.at[k])

    def update(k):
        r0 = k * NB
        first = first_block(k, count)
        fetch(k).wait()
        for j in range(k, count):
            r_ref[r0 : r0 + NB, j * NB : (j + 1) * NB] = g_ref[first + j - k] * scale
        if k > 0:
            r_ref[r0 : r0 + NB, r0:] -= lax.dot_general(
                r_ref[0:r0, r0 : r0 + NB], r_ref[0:r0, r0:], (((0,), (0,)), ((), ())), **DOT
            )
        d_ref[...] = r_ref[r0 : r0 + NB, r0 : r0 + NB]

    def panel(k):
        r0 = k * NB
        r_ref[r0 : r0 + NB, r0 : r0 + NB] = d_ref[...]
        if k + 1 < count:
            r_ref[r0 : r0 + NB, r0 + NB :] = lax.dot_general(
                w_ref[...], r_ref[r0 : r0 + NB, r0 + NB :], (((1,), (0,)), ((), ())), **DOT
            )
        leave(k).start()

    def step(k, _):
        lax.switch(k, [functools.partial(update, i) for i in range(count)])
        rows, inv = factor_block([d_ref[8 * i : 8 * i + 8, :] for i in range(NB // 8)])
        for i in range(NB // 8):
            d_ref[8 * i : 8 * i + 8, :] = rows[i]
            w_ref[8 * i : 8 * i + 8, :] = inv[i]
        lax.switch(k, [functools.partial(panel, i) for i in range(count)])
        return 0

    lax.fori_loop(0, count, step, 0)
    for k in range(count):
        leave(k).wait()


def upper_factor(blocks, count, scale):
    size = count * NB
    return pl.pallas_call(
        functools.partial(factor_body, count, scale),
        out_shape=jax.ShapeDtypeStruct((size, size), F32),
        in_specs=[pl.BlockSpec(memory_space=pltpu.HBM)],
        out_specs=pl.BlockSpec(memory_space=pltpu.HBM),
        scratch_shapes=[pltpu.VMEM(blocks.shape, F32), pltpu.VMEM((size, size), F32), pltpu.VMEM((NB, NB), F32),
                        pltpu.VMEM((NB, NB), F32), pltpu.SemaphoreType.DMA((2 * count,))],
        compiler_params=pltpu.CompilerParams(vmem_limit_bytes=48 << 20),
    )(blocks)


def on_device(signals, channel_node, lag_offsets):
    total_rows = signals.shape[0] * lax.axis_size("tm")
    count = lag_offsets.shape[0] * NODES // NB
    blocks = gram_blocks(signals, channel_node, lag_offsets)
    return upper_factor(blocks, count, 1.0 / total_rows)


def solution(mesh):
    in_specs = (P("tm", "chan"), P("chan"), P())
    out_specs = P()
    return jax.shard_map(
        on_device, mesh=mesh, in_specs=in_specs, out_specs=out_specs, check_vma=False
    )
```

time: 647 us -> 117 us (0.18)
  waiting for transfers between devices: 303 us -> 0 us
  other arithmetic: 190 us -> 0 us
  Pallas kernels: 0 us -> 115 us
  blocking collectives: 51.9 us -> 0 us
  matrix products: 43 us -> 0 us
  between operations: 33.6 us -> 0.18 us
  local copies, waits for them, and re-layouts: 16.9 us -> 1.66 us
    psum x1 -> x0, waiting for transfers between devices: 267 us -> none  [on_device(): gram_matrix = lax.psum(local_gram, ('tm', 'chan'))]
    another operation x30 -> x0, other arithmetic: 172 us -> none  [on_device(): return jnp.linalg.cholesky(gram_matrix / row_total).T]
    pallas_call x0 -> x2, Pallas kernels: none -> 115 us  [the longest x1 81.9 us: gram_blocks(): pl.pallas_call(functools.partial(gram_body, lags.shape[0]), out_shape=jax...]
    all_to_all x1 -> x0, blocking collectives: 51.9 us -> none  [on_device(): lax.all_to_all(panel, 'chan', split_axis=0, concat_axis=1, tiled=True)]
    reduce_scatter x1 -> x0, waiting for transfers between devices: 36.2 us -> none  [on_device(): lax.psum_scatter(partial_value, 'chan', scatter_dimension=1, tiled=True)]
    another operation x14 -> x0, matrix products: 22.9 us -> none  [on_device(): return jnp.linalg.cholesky(gram_matrix / row_total).T]
    dot_general x2 -> x0, matrix products: 20 us -> none  [the longest x1 14.9 us: on_device(): lax.dot_general(hankel, hankel, (((0,), (0,)), ((), ())), precision=lax.P...]
    div x2 -> x0, other arithmetic: 9.49 us -> none  [on_device(): return jnp.linalg.cholesky(gram_matrix / row_total).T]
  transfers between devices with their start and end apart: 3 -> 0, of which waited for: 2 -> 0; matrix products, arithmetic and copies ran while one was open for 0% -> 0% of each run, Pallas kernels for 0% -> 0%
where the time goes in v5:
time: 117 us
  Pallas kernels  115 us (98%)
  local copies, waits for them, and re-layouts  1.66 us (1%)
    pallas_call x1, Pallas kernels, gram_blocks(): pl.pallas_call(functools.partial(gram_body, lags.shape[0]), out_shape=jax...  81.9 us
    pallas_call x1, Pallas kernels, upper_factor(): pl.pallas_call(functools.partial(factor_body, count, scale), out_shape=ja...  33.2 us

profile of v5, /device:TPU:1, one launch (start us, length us, event | category | flops | bytes accessed | tf_op | source)
XLA Modules:
  0.0 117.0 jit_solution(3961566155400469355)
XLA Ops:
  0.0 81.9 %shard_map.37 = f32[576,8,128]{2,1,0:T(8,128)} custom-call(s32[8]{0:T(128)} %lags_ref.1, bf16[4096,512]{1,0:T(8,128)(2,1)} %s_hbm.1, s32[1,512]{1,0:T(1,128)} %bitcast.3), custom_call_target="tpu_custom_call" | custom-call | tf_op jit(solution)/shard_map/pallas_call | solution.py:364
  81.9 0.0 copy-start
  81.9 1.7 %copy-done = f32[576,8,128]{2,1,0:T(8,128)S(1)} copy-done((f32[576,8,128]{2,1,0:T(8,128)S(1)}, f32[576,8,128]{2,1,0:T(8,128)}, u32[]{:S(2)}) %copy-start) | copy-done | bytes 2359320
  83.6 33.2 %shard_map.38 = f32[1024,1024]{1,0:T(8,128)} custom-call(f32[36,128,128]{2,1,0:T(8,128)S(1)} %bitcast.2), custom_call_target="tpu_custom_call" | custom-call | tf_op jit(solution)/shard_map/pallas_call | solution.py:504
Async XLA Ops:
  81.9 1.7 %copy-start = (f32[576,8,128]{2,1,0:T(8,128)S(1)}, f32[576,8,128]{2,1,0:T(8,128)}, u32[]{:S(2)}) copy-start(f32[576,8,128]{2,1,0:T(8,128)} %shard_map.37) | copy-start | bytes 7077892

commit v6 on v5

--- a/solution.py
+++ b/solution.py
@@ -17,7 +17,7 @@
 VMEM = pl.BlockSpec(memory_space=pltpu.VMEM)
 NB = 128
 NX, NY, NZ = 4, 4, 8
-SEGMENTS = 3
+SEGMENTS = 1
 OWNERS = 6
 
 

time: 117 us -> 115 us (0.983)
  Pallas kernels: 115 us -> 113 us
    pallas_call x1, Pallas kernels: 81.9 us -> 79.7 us  [gram_blocks(): pl.pallas_call(functools.partial(gram_body, lags.shape[0]), out_shape=jax...]
where the time goes in v6:
time: 115 us
  Pallas kernels  113 us (98%)
  local copies, waits for them, and re-layouts  1.66 us (1%)
    pallas_call x1, Pallas kernels, gram_blocks(): pl.pallas_call(functools.partial(gram_body, lags.shape[0]), out_shape=jax...  79.7 us
    pallas_call x1, Pallas kernels, upper_factor(): pl.pallas_call(functools.partial(factor_body, count, scale), out_shape=ja...  33.2 us

profile of v6, /device:TPU:1, one launch (start us, length us, event | category | flops | bytes accessed | tf_op | source)
XLA Modules:
  0.0 114.8 jit_solution(6288327737788515209)
XLA Ops:
  0.0 79.7 %shard_map.37 = f32[576,8,128]{2,1,0:T(8,128)} custom-call(s32[8]{0:T(128)} %lags_ref.1, bf16[4096,512]{1,0:T(8,128)(2,1)} %s_hbm.1, s32[1,512]{1,0:T(1,128)} %bitcast.3), custom_call_target="tpu_custom_call" | custom-call | tf_op jit(solution)/shard_map/pallas_call | solution.py:364
  79.7 0.0 copy-start
  79.8 1.7 %copy-done = f32[576,8,128]{2,1,0:T(8,128)S(1)} copy-done((f32[576,8,128]{2,1,0:T(8,128)S(1)}, f32[576,8,128]{2,1,0:T(8,128)}, u32[]{:S(2)}) %copy-start) | copy-done | bytes 2359320
  81.4 33.2 %shard_map.38 = f32[1024,1024]{1,0:T(8,128)} custom-call(f32[36,128,128]{2,1,0:T(8,128)S(1)} %bitcast.2), custom_call_target="tpu_custom_call" | custom-call | tf_op jit(solution)/shard_map/pallas_call | solution.py:504
Async XLA Ops:
  79.7 1.7 %copy-start = (f32[576,8,128]{2,1,0:T(8,128)S(1)}, f32[576,8,128]{2,1,0:T(8,128)}, u32[]{:S(2)}) copy-start(f32[576,8,128]{2,1,0:T(8,128)} %shard_map.37) | copy-start | bytes 7077892

commit v7 on v6

--- a/solution.py
+++ b/solution.py
@@ -173,9 +173,11 @@
         value = lax.dot_general(a, lo[at, i * NB :], dims, preferred_element_type=F32)
         value += lax.dot_general(d, hi[at, i * NB :], dims, preferred_element_type=F32)
         value += lax.dot_general(a, hi[at, i * NB :], dims, preferred_element_type=F32)
+        square = lax.dot_general(d, d, dims, preferred_element_type=F32)
         for j in range(i, count):
             spot = 16 * (first_block(i, count) + j - i)
-            block = value[:, (j - i) * NB : (j - i + 1) * NB].reshape(16, 8, NB)
+            block = value[:, (j - i) * NB : (j - i + 1) * NB]
+            block = (block + square if j == i else block).reshape(16, 8, NB)
             g[spot : spot + 16] = g[spot : spot + 16] + block if add else block
 
     for r in range(per_tile):
@@ -383,6 +385,9 @@
     return total.reshape(blocks, NB, NB)
 
 
+DOT = dict(precision=lax.Precision.HIGHEST, preferred_element_type=F32)
+
+
 def lanes(x, c):
     return jnp.broadcast_to(x[:, c : c + 1], x.shape)
 
@@ -396,15 +401,22 @@
     lane = lax.broadcasted_iota(jnp.int32, (8, NB), 1)
     sub = lax.broadcasted_iota(jnp.int32, (8, NB), 0)
     rows = list(rows)
-    upper, inv = [], []
+    upper, inv, merged = [], [], []
     cur = [lanes(rows[0], j) for j in range(8)]
     for p in range(count):
         r0 = 8 * p
-        raw = {b: [lanes(rows[b], r0 + j) for j in range(8)] for b in range(p + 1, count)}
-        ahead = [lanes(rows[p + 1], r0 + 8 + j) for j in range(8)] if p + 1 < count else None
+        end = count // 2 if p < count // 2 else count
+        if p == count // 2:
+            above = jnp.concatenate(merged, axis=0)
+            product = lax.dot_general(above, above, (((0,), (0,)), ((), ())), **DOT)
+            for b in range(p, count):
+                rows[b] = jnp.where(lane >= r0, rows[b], 0.0) - product[8 * b : 8 * b + 8]
+            cur = [lanes(rows[p], r0 + j) for j in range(8)]
+        raw = {b: [lanes(rows[b], r0 + j) for j in range(8)] for b in range(p + 1, end)}
+        ahead = [lanes(rows[p + 1], r0 + 8 + j) for j in range(8)] if p + 1 < end else None
         here = jnp.logical_and(lane >= r0, lane < r0 + 8)
         top, low = rows[p], jnp.where(here, jnp.where(lane == sub + r0, 1.0, 0.0), rows[p])
-        for b in range(p + 1, count):
+        for b in range(p + 1, end):
             rows[b] = jnp.where(here, 0.0, rows[b])
         v, m, s, rinv = list(cur), [None] * 8, [[None] * 8 for _ in range(8)], [None] * 8
         diag = None
@@ -426,7 +438,7 @@
             da = subs(top, j)
             low = low - m[j] * ra[j]
             top = top - m[j] * da
-        for b in range(p + 1, count):
+        for b in range(p + 1, end):
             u, mb = [], []
             for j in range(8):
                 value = raw[b][j]
@@ -445,10 +457,8 @@
                 rows[b] = rows[b] - mb[j] * ra[j]
         upper.append(jnp.where(lane >= sub + r0, top * rs, 0.0))
         inv.append(jnp.where(lane < r0 + 8, low * rs, 0.0))
+        merged.append(jnp.where(lane < NB // 2, inv[-1], upper[-1]))
     return upper, inv
-
-
-DOT = dict(precision=lax.Precision.HIGHEST, preferred_element_type=F32)
 
 
 def factor_body(count, scale, g_hbm, out_hbm, g_ref, r_ref, w_ref, d_ref, sem):
@@ -508,7 +518,7 @@
         out_specs=pl.BlockSpec(memory_space=pltpu.HBM),
         scratch_shapes=[pltpu.VMEM(blocks.shape, F32), pltpu.VMEM((size, size), F32), pltpu.VMEM((NB, NB), F32),
                         pltpu.VMEM((NB, NB), F32), pltpu.SemaphoreType.DMA((2 * count,))],
-        compiler_params=pltpu.CompilerParams(vmem_limit_bytes=48 << 20),
+        compiler_params=pltpu.CompilerParams(vmem_limit_bytes=63_000_000),
     )(blocks)
 
 

time: 115 us -> 110 us (0.957)
  Pallas kernels: 113 us -> 110 us
  local copies, waits for them, and re-layouts: 1.66 us -> 0 us
    pallas_call x1, Pallas kernels: 33.2 us -> 29.3 us  [upper_factor(): pl.pallas_call(functools.partial(factor_body, count, scale), out_shape=ja...]
    unnamed x2 -> x0, local copies, waits for them, and re-layouts: 1.66 us -> none
where the time goes in v7:
time: 110 us
  Pallas kernels  110 us (100%)
    pallas_call x1, Pallas kernels, gram_blocks(): pl.pallas_call(functools.partial(gram_body, lags.shape[0]), out_shape=jax...  80.4 us
    pallas_call x1, Pallas kernels, upper_factor(): pl.pallas_call(functools.partial(factor_body, count, scale), out_shape=ja...  29.3 us

profile of v7, /device:TPU:1, one launch (start us, length us, event | category | flops | bytes accessed | tf_op | source)
XLA Modules:
  0.0 109.8 jit_solution(11344279934006014164)
XLA Ops:
  0.0 80.4 %shard_map.37 = f32[576,8,128]{2,1,0:T(8,128)} custom-call(s32[8]{0:T(128)} %lags_ref.1, bf16[4096,512]{1,0:T(8,128)(2,1)} %s_hbm.1, s32[1,512]{1,0:T(1,128)} %bitcast.3), custom_call_target="tpu_custom_call" | custom-call | tf_op jit(solution)/shard_map/pallas_call | solution.py:366
  80.4 29.3 %shard_map.38 = f32[1024,1024]{1,0:T(8,128)} custom-call(f32[36,128,128]{2,1,0:T(8,128)} %bitcast.2), custom_call_target="tpu_custom_call" | custom-call | tf_op jit(solution)/shard_map/pallas_call | solution.py:514

commit v8 on v7

--- a/solution.py
+++ b/solution.py
@@ -204,8 +204,8 @@
     color_part = side // 2
     ring_part = color_part // 4
     small = ring_part // 4
-    sems = iter(range(SEGMENTS * 42))
-    ids = [[[next(sems) for _ in range(n)] for n in (2, 6, 6, 7, 7, 6, 6, 2)] for _ in range(SEGMENTS)]
+    sems = iter(range(SEGMENTS * 54))
+    ids = [[[next(sems) for _ in range(n)] for n in (8, 6, 6, 7, 7, 6, 6, 8)] for _ in range(SEGMENTS)]
 
     def ring(color, d, first):
         if (color == 0) == first:
@@ -227,34 +227,43 @@
         stages[s][stage].append(cp)
         plain.append(cp)
 
+    far_first = (2, 1, 3)
+
     def cores(s):
-        for color in range(2):
-            at = pl.ds(s * units + (1 - c) * side + color * color_part, color_part)
-            go(s, 0, send_to(g.at[at], rc.at[s, color], s, 0, color, partner))
+        for n, d in enumerate(far_first + (0,)):
+            for color in range(2):
+                part_at = pl.ds(ring(color, d, True)[1] * ring_part, ring_part)
+                first = s * units + (1 - c) * side + color * color_part
+                at = pl.ds(first + ring(color, d, True)[1] * ring_part, ring_part)
+                go(s, 0, send_to(g.at[at], rc.at[s, color, part_at], s, 0, 2 * n + color, partner))
 
     def ring_first(s):
-        for color in range(2):
-            stages[s][0][color].wait_recv()
-            at = pl.ds(s * units + c * side + color * color_part, color_part)
-            h[s, color] = g[at] + rc[s, color]
-            for d in range(1, 4):
+        for n, d in enumerate(far_first + (0,)):
+            for color in range(2):
+                stages[s][0][2 * n + color].wait_recv()
                 dev, spot = ring(color, d, True)
-                go(s, 1, send_to(h.at[s, color, pl.ds(spot * ring_part, ring_part)],
-                                 ra.at[s, color, d - 1], s, 1, 3 * color + d - 1, dev))
+                part_at = pl.ds(spot * ring_part, ring_part)
+                at = pl.ds(s * units + c * side + color * color_part + spot * ring_part, ring_part)
+                h[s, color, part_at] = g[at] + rc[s, color, part_at]
+                if d > 0:
+                    go(s, 1, send_to(h.at[s, color, part_at], ra.at[s, color, d - 1],
+                                     s, 1, 3 * color + d - 1, dev))
 
     def ring_second(s):
         for color in range(2):
-            for cp in stages[s][1][3 * color : 3 * color + 3]:
+            for cp in stages[s][1][color::2]:
                 cp.wait_recv()
             _, spot = ring(color, 0, True)
             sa[s, color] = ((h[s, color, pl.ds(spot * ring_part, ring_part)] + ra[s, color, 0])
                             + (ra[s, color, 1] + ra[s, color, 2]))
-            for d in range(1, 4):
+            for d in far_first:
                 dev, spot = ring(color, d, False)
                 go(s, 2, send_to(sa.at[s, color, pl.ds(spot * small, small)],
                                  rb.at[s, color, d - 1], s, 2, 3 * color + d - 1, dev))
 
     size = 2 * small // OWNERS
+    z_order = (4, 3, 5, 2, 6, 1, 7)
+    to_z, from_z = [{} for _ in range(SEGMENTS)], [{} for _ in range(SEGMENTS)]
     mine = jnp.minimum(z, OWNERS - 1)
 
     def along_z(s):
@@ -265,12 +274,12 @@
             ys[s, color * small : (color + 1) * small] = (
                 (sa[s, color, pl.ds(spot * small, small)] + rb[s, color, 0])
                 + (rb[s, color, 1] + rb[s, color, 2]))
-        for d in range(1, NZ):
+        for d in z_order:
             dst = lax.rem(z + d, NZ)
             at = pl.ds(jnp.minimum(dst, OWNERS - 1) * size, size)
             cp = send_to(ys.at[s, at], rz.at[s, d - 1], s, 3, d - 1, device(x, y, dst, c))
             pl.when(dst < OWNERS)(cp.start)
-            stages[s][3].append(cp)
+            to_z[s][d] = cp
 
     def spot_of(s, p):
         color = p // (OWNERS // 2)
@@ -284,26 +293,26 @@
         @pl.when(z < OWNERS)
         def _():
             total = ys[s, pl.ds(mine * size, size)]
-            for d in range(1, NZ):
-                stages[s][3][d - 1].wait_recv()
+            for d in reversed(z_order):
+                to_z[s][d].wait_recv()
                 total = total + rz[s, d - 1]
             out_ref[at] = total
 
-        for d in range(1, NZ):
+        for d in z_order:
             cp = send_to(out_ref.at[at], out_ref.at[at], s, 4, d - 1,
                          device(x, y, lax.rem(z + d, NZ), c))
             pl.when(z < OWNERS)(cp.start)
-            stages[s][4].append(cp)
+            from_z[s][d] = cp
 
     def back_second(s):
         for d in range(1, NZ):
-            pl.when(lax.rem(z - d + NZ, NZ) < OWNERS)(stages[s][4][d - 1].wait_recv)
+            pl.when(lax.rem(z - d + NZ, NZ) < OWNERS)(from_z[s][d].wait_recv)
         for color in range(2):
             _, spot = ring(color, 0, True)
             _, sub = ring(color, 0, False)
             at = pl.ds(s * units + c * side + color * color_part + spot * ring_part + sub * small,
                        small)
-            for d in range(1, 4):
+            for d in far_first:
                 dev, _ = ring(color, d, False)
                 go(s, 5, send_to(out_ref.at[at], out_ref.at[at], s, 5, 3 * color + d - 1, dev))
 
@@ -313,27 +322,41 @@
                 cp.wait_recv()
             _, spot = ring(color, 0, True)
             at = pl.ds(s * units + c * side + color * color_part + spot * ring_part, ring_part)
-            for d in range(1, 4):
+            for d in far_first:
                 dev, _ = ring(color, d, True)
                 go(s, 6, send_to(out_ref.at[at], out_ref.at[at], s, 6, 3 * color + d - 1, dev))
 
+    def hand_over(s, color, d):
+        _, spot = ring(color, (4 - d) % 4, True)
+        at = pl.ds(s * units + c * side + color * color_part + spot * ring_part, ring_part)
+        go(s, 7, send_to(out_ref.at[at], out_ref.at[at], s, 7, 4 * color + d, partner))
+
     def back_cores(s):
         for color in range(2):
-            for cp in stages[s][6][3 * color : 3 * color + 3]:
-                cp.wait_recv()
-            at = pl.ds(s * units + c * side + color * color_part, color_part)
-            go(s, 7, send_to(out_ref.at[at], out_ref.at[at], s, 7, color, partner))
+            hand_over(s, color, 0)
+        for d in (1, 3, 2):
+            for color in range(2):
+                stages[s][6][3 * color + far_first.index(d)].wait_recv()
+                hand_over(s, color, d)
 
     def last(s):
         for cp in stages[s][7]:
             cp.wait_recv()
 
-    done = 0
-    for s in range(SEGMENTS):
-        while first_block(done, count) * 16 < (s + 1) * units:
-            products(done, slice(half, rows), True)
-            done += 1
-        cores(s)
+    cut = next(r for r in range(count) if 2 * first_block(r + 1, count) > first_block(count, count))
+    late = slice(half, rows)
+
+    def some(core, first, stop):
+        @pl.when(c == core)
+        def _():
+            for i in range(first, stop):
+                products(i, late, True)
+
+    some(0, cut, count)
+    some(1, 0, cut + 1)
+    cores(0)
+    some(0, 0, cut)
+    some(1, cut + 1, count)
     chain = (ring_first, ring_second, along_z, back_z, back_second, back_first, back_cores, last)
     for slot in range(len(chain) + SEGMENTS - 1):
         for s in range(SEGMENTS):
@@ -348,8 +371,8 @@
         cp.wait_send()
     for s in range(SEGMENTS):
         for d in range(1, NZ):
-            pl.when(lax.rem(z + d, NZ) < OWNERS)(stages[s][3][d - 1].wait_send)
-            pl.when(z < OWNERS)(stages[s][4][d - 1].wait_send)
+            pl.when(lax.rem(z + d, NZ) < OWNERS)(to_z[s][d].wait_send)
+            pl.when(z < OWNERS)(from_z[s][d].wait_send)
 
 
 def gram_blocks(signals, channel_node, lags):
@@ -377,7 +400,7 @@
             tiles(blocks * 16), tiles(S, 2, side // 2), tiles(S, 2, side // 2),
             tiles(S, 2, 3, side // 8), tiles(S, 2, side // 8), tiles(S, 2, 3, side // 32),
             tiles(S, side // 16), tiles(S, NZ - 1, side // 16 // OWNERS),
-            dma((8,)), dma((13,)), dma((13,)), dma((S * 42,)), dma((S * 42,)),
+            dma((8,)), dma((13,)), dma((13,)), dma((S * 54,)), dma((S * 54,)),
         ],
         compiler_params=pltpu.CompilerParams(
             collective_id=1, has_side_effects=True, vmem_limit_bytes=56 << 20),

time: 110 us -> 108 us (0.982)
  Pallas kernels: 110 us -> 108 us
    pallas_call x1, Pallas kernels: 80.4 us -> 78.4 us  [gram_blocks(): pl.pallas_call(functools.partial(gram_body, lags.shape[0]), out_shape=jax...]
where the time goes in v8:
time: 108 us
  Pallas kernels  108 us (100%)
    pallas_call x1, Pallas kernels, gram_blocks(): pl.pallas_call(functools.partial(gram_body, lags.shape[0]), out_shape=jax...  78.4 us
    pallas_call x1, Pallas kernels, upper_factor(): pl.pallas_call(functools.partial(factor_body, count, scale), out_shape=ja...  29.2 us

profile of v8, /device:TPU:1, one launch (start us, length us, event | category | flops | bytes accessed | tf_op | source)
XLA Modules:
  0.0 107.9 jit_solution(17258690591209744965)
XLA Ops:
  0.0 78.4 %shard_map.37 = f32[576,8,128]{2,1,0:T(8,128)} custom-call(s32[8]{0:T(128)} %lags_ref.1, bf16[4096,512]{1,0:T(8,128)(2,1)} %s_hbm.1, s32[1,512]{1,0:T(1,128)} %bitcast.3), custom_call_target="tpu_custom_call" | custom-call | tf_op jit(solution)/shard_map/pallas_call | solution.py:389
  78.4 29.2 %shard_map.38 = f32[1024,1024]{1,0:T(8,128)} custom-call(f32[36,128,128]{2,1,0:T(8,128)} %bitcast.2), custom_call_target="tpu_custom_call" | custom-call | tf_op jit(solution)/shard_map/pallas_call | solution.py:537

commit v9 on v8

--- a/solution.py
+++ b/solution.py
@@ -497,17 +497,29 @@
         at = pl.ds(k * NB, NB)
         return pltpu.make_async_copy(r_ref.at[at], out_hbm.at[at], sem.at[k])
 
-    def update(k):
-        r0 = k * NB
-        first = first_block(k, count)
+    def take(k, less):
         fetch(k).wait()
         for j in range(k, count):
-            r_ref[r0 : r0 + NB, j * NB : (j + 1) * NB] = g_ref[first + j - k] * scale
-        if k > 0:
-            r_ref[r0 : r0 + NB, r0:] -= lax.dot_general(
-                r_ref[0:r0, r0 : r0 + NB], r_ref[0:r0, r0:], (((0,), (0,)), ((), ())), **DOT
-            )
-        d_ref[...] = r_ref[r0 : r0 + NB, r0 : r0 + NB]
+            value = g_ref[first_block(k, count) + j - k] * scale
+            if less is not None:
+                value = value - less[:, (j - k) * NB : (j - k + 1) * NB]
+            r_ref[k * NB : (k + 1) * NB, j * NB : (j + 1) * NB] = value
+
+    def update(k):
+        r0, r1 = k * NB, (k + 1) * NB
+        if k % 2 == 0:
+            less = [None, None]
+            if k > 0:
+                both = lax.dot_general(r_ref[0:r0, r0 : r1 + NB], r_ref[0:r0, r0:],
+                                       (((0,), (0,)), ((), ())), **DOT)
+                less = [both[:NB], both[NB:, NB:]]
+            take(k, less[0])
+            take(k + 1, less[1])
+        else:
+            r_ref[r0:r1, r0:] -= lax.dot_general(
+                r_ref[r0 - NB : r0, r0:r1], r_ref[r0 - NB : r0, r0:],
+                (((0,), (0,)), ((), ())), **DOT)
+        d_ref[...] = r_ref[r0:r1, r0:r1]
 
     def panel(k):
         r0 = k * NB

time: 108 us -> 108 us (level)
  no operation moved by 1% of the time
where the time goes in v9:
time: 108 us
  Pallas kernels  108 us (100%)
    pallas_call x1, Pallas kernels, gram_blocks(): pl.pallas_call(functools.partial(gram_body, lags.shape[0]), out_shape=jax...  78.4 us
    pallas_call x1, Pallas kernels, upper_factor(): pl.pallas_call(functools.partial(factor_body, count, scale), out_shape=ja...  29.5 us

profile of v9, /device:TPU:1, one launch (start us, length us, event | category | flops | bytes accessed | tf_op | source)
XLA Modules:
  0.0 108.1 jit_solution(16012293609660968601)
XLA Ops:
  0.0 78.4 %shard_map.37 = f32[576,8,128]{2,1,0:T(8,128)} custom-call(s32[8]{0:T(128)} %lags_ref.1, bf16[4096,512]{1,0:T(8,128)(2,1)} %s_hbm.1, s32[1,512]{1,0:T(1,128)} %bitcast.3), custom_call_target="tpu_custom_call" | custom-call | tf_op jit(solution)/shard_map/pallas_call | solution.py:389
  78.4 29.5 %shard_map.38 = f32[1024,1024]{1,0:T(8,128)} custom-call(f32[36,128,128]{2,1,0:T(8,128)} %bitcast.2), custom_call_target="tpu_custom_call" | custom-call | tf_op jit(solution)/shard_map/pallas_call | solution.py:549

commit v10 on v9

--- a/solution.py
+++ b/solution.py
@@ -36,9 +36,9 @@
     )
 
 
-def gram_body(lag_count, lags_ref, s_hbm, node_ref, out_ref,
+def gram_body(lag_count, lags_ref, s_hbm, node_ref, out_hbm,
               sig, part, far, near, pair, fwd, own, land, rot, hi, lo,
-              g, rc, h, ra, sa, rb, ys, rz, load, send, recv, ssend, srecv):
+              g, rc, h, ra, sa, rb, ys, rz, out_ref, load, send, recv, ssend, srecv, leaves):
     x, t = lax.axis_index("chan"), lax.axis_index("tm")
     y, z, c = t // (NZ * 2), lax.rem(t // 2, NZ), lax.rem(t, 2)
     rows = own.shape[0]
@@ -326,10 +326,21 @@
                 dev, _ = ring(color, d, True)
                 go(s, 6, send_to(out_ref.at[at], out_ref.at[at], s, 6, 3 * color + d - 1, dev))
 
+    def part_at(s, core, color, d):
+        _, spot = ring(color, (4 - d) % 4, True)
+        return pl.ds(s * units + core * side + color * color_part + spot * ring_part, ring_part)
+
+    left = []
+
+    def leave(at):
+        cp = pltpu.make_async_copy(out_ref.at[at], out_hbm.at[at], leaves.at[len(left)])
+        cp.start()
+        left.append(cp)
+
     def hand_over(s, color, d):
-        _, spot = ring(color, (4 - d) % 4, True)
-        at = pl.ds(s * units + c * side + color * color_part + spot * ring_part, ring_part)
+        at = part_at(s, c, color, d)
         go(s, 7, send_to(out_ref.at[at], out_ref.at[at], s, 7, 4 * color + d, partner))
+        leave(at)
 
     def back_cores(s):
         for color in range(2):
@@ -340,8 +351,12 @@
                 hand_over(s, color, d)
 
     def last(s):
-        for cp in stages[s][7]:
-            cp.wait_recv()
+        for n, d in enumerate((0, 1, 3, 2)):
+            for color in range(2):
+                stages[s][7][2 * n + color].wait_recv()
+                leave(part_at(s, 1 - c, color, d))
+        for cp in left:
+            cp.wait()
 
     cut = next(r for r in range(count) if 2 * first_block(r + 1, count) > first_block(count, count))
     late = slice(half, rows)
@@ -390,7 +405,7 @@
         functools.partial(gram_body, lags.shape[0]),
         out_shape=jax.ShapeDtypeStruct((blocks * 16, 8, NB), F32),
         in_specs=[pl.BlockSpec(memory_space=pltpu.SMEM), pl.BlockSpec(memory_space=pl.ANY), VMEM],
-        out_specs=VMEM,
+        out_specs=pl.BlockSpec(memory_space=pltpu.HBM),
         scratch_shapes=[
             pltpu.VMEM((length, chans), BF16), pltpu.VMEM((length, NODES), F32),
             quarters, quarters, quarters, quarters,
@@ -400,7 +415,8 @@
             tiles(blocks * 16), tiles(S, 2, side // 2), tiles(S, 2, side // 2),
             tiles(S, 2, 3, side // 8), tiles(S, 2, side // 8), tiles(S, 2, 3, side // 32),
             tiles(S, side // 16), tiles(S, NZ - 1, side // 16 // OWNERS),
-            dma((8,)), dma((13,)), dma((13,)), dma((S * 54,)), dma((S * 54,)),
+            tiles(blocks * 16),
+            dma((8,)), dma((13,)), dma((13,)), dma((S * 54,)), dma((S * 54,)), dma((16,)),
         ],
         compiler_params=pltpu.CompilerParams(
             collective_id=1, has_side_effects=True, vmem_limit_bytes=56 << 20),

time: 108 us -> 108 us (level)
  no operation moved by 1% of the time
where the time goes in v10:
time: 108 us
  Pallas kernels  107 us (99%)
    pallas_call x1, Pallas kernels, gram_blocks(): pl.pallas_call(functools.partial(gram_body, lags.shape[0]), out_shape=jax...  77.9 us
    pallas_call x1, Pallas kernels, upper_factor(): pl.pallas_call(functools.partial(factor_body, count, scale), out_shape=ja...  29.5 us

profile of v10, /device:TPU:1, one launch (start us, length us, event | category | flops | bytes accessed | tf_op | source)
XLA Modules:
  0.0 107.5 jit_solution(16437866222174033111)
XLA Ops:
  0.0 77.9 %shard_map.37 = f32[576,8,128]{2,1,0:T(8,128)} custom-call(s32[8]{0:T(128)} %lags_ref.1, bf16[4096,512]{1,0:T(8,128)(2,1)} %s_hbm.1, s32[1,512]{1,0:T(1,128)} %bitcast.3), custom_call_target="tpu_custom_call" | custom-call | tf_op jit(solution)/shard_map/pallas_call | solution.py:404
  77.9 29.5 %shard_map.38 = f32[1024,1024]{1,0:T(8,128)} custom-call(f32[36,128,128]{2,1,0:T(8,128)} %bitcast.2), custom_call_target="tpu_custom_call" | custom-call | tf_op jit(solution)/shard_map/pallas_call | solution.py:565

commit v11 on v10

--- a/solution.py
+++ b/solution.py
@@ -530,8 +530,11 @@
                                        (((0,), (0,)), ((), ())), **DOT)
                 less = [both[:NB], both[NB:, NB:]]
             take(k, less[0])
-            take(k + 1, less[1])
+            if k > 0:
+                take(k + 1, less[1])
         else:
+            if k == 1:
+                take(k, None)
             r_ref[r0:r1, r0:] -= lax.dot_general(
                 r_ref[r0 - NB : r0, r0:r1], r_ref[r0 - NB : r0, r0:],
                 (((0,), (0,)), ((), ())), **DOT)

time: 108 us -> 107 us (level)
  no operation moved by 1% of the time
where the time goes in v11:
time: 107 us
  Pallas kernels  107 us (100%)
    pallas_call x1, Pallas kernels, gram_blocks(): pl.pallas_call(functools.partial(gram_body, lags.shape[0]), out_shape=jax...  77.8 us
    pallas_call x1, Pallas kernels, upper_factor(): pl.pallas_call(functools.partial(factor_body, count, scale), out_shape=ja...  29.4 us

profile of v11, /device:TPU:1, one launch (start us, length us, event | category | flops | bytes accessed | tf_op | source)
XLA Modules:
  0.0 107.3 jit_solution(5810440089889456768)
XLA Ops:
  0.0 77.8 %shard_map.37 = f32[576,8,128]{2,1,0:T(8,128)} custom-call(s32[8]{0:T(128)} %lags_ref.1, bf16[4096,512]{1,0:T(8,128)(2,1)} %s_hbm.1, s32[1,512]{1,0:T(1,128)} %bitcast.3), custom_call_target="tpu_custom_call" | custom-call | tf_op jit(solution)/shard_map/pallas_call | solution.py:404
  77.8 29.4 %shard_map.38 = f32[1024,1024]{1,0:T(8,128)} custom-call(f32[36,128,128]{2,1,0:T(8,128)} %bitcast.2), custom_call_target="tpu_custom_call" | custom-call | tf_op jit(solution)/shard_map/pallas_call | solution.py:568
